TPU v7x, 32 devices: a whole 2x2x4 slice. The times are simulated.
32 devices in a mesh: pop: 8 (over z, x), grp: 4 (over y, core).
Axes of the slice: x: 2, y: 2, z: 4, core: 2. Of those that a mesh axis runs over, the one named last changes fastest.
Arguments:
- actions: bfloat16 [16384, 1024], P(('pop', 'grp')), may hold values from -6 to 6
- elite_mask: int32 [16384], P(('pop', 'grp')), may hold values from 0 to 1, as said below
- init_state: float32 [256], replicated, may hold values from -6 to 6
- w_state: bfloat16 [256, 256], replicated, may hold values from -0.375 to 0.375
- w_action: bfloat16 [32, 256], replicated, may hold values from -1 to 1
- bias: float32 [256], replicated, may hold values from -3 to 3
- w_out: bfloat16 [256, 256], replicated, may hold values from -0.375 to 0.375
- reward_vec: float32 [256], replicated, may hold values from -0.375 to 0.375
Outputs:
- new_mean: float32 [1024], replicated
- covariance: float32 [1024, 1024], P('pop')
- returns: float32 [16384], P(('pop', 'grp'))
Inputs may be any that keep to these rules, and one draw needn't show every extreme that they name: `elite_mask`: each aligned block of 512 candidates (the candidates of one device) holds at least one elite.
All inputs are finite; a program needn't handle non-finite values.
Results may differ from a plain program's by a relative error of at most 0.0063.
Values sent between devices are 32-bit elements; how exact they have to be, the bound alone decides.
No kernel may reach another device: no remote copies, remote signals or barrier semaphores. Data moves between devices by JAX's collectives and lax.ppermute only.
A program may use at most 64 MiB of HBM per device.

v0:
```python
import functools

import jax
import jax.numpy as jnp
from jax import lax
from jax.experimental import pallas as pl
from jax.experimental.pallas import tpu as pltpu
from jax.sharding import PartitionSpec as P

ALL = ("pop", "grp")
CORE = (("grp", 1), ("grp", 1))
VMEM = pl.BlockSpec(memory_space=pltpu.VMEM)
SMEM = pl.BlockSpec(memory_space=pltpu.SMEM)
HBM = pl.BlockSpec(memory_space=pltpu.HBM)
PIECES = (4, 4, 4, 4, 4, 4, 4, 4)


def bits_of(size):
    return [1 << k for k in range(size.bit_length() - 1)]


class Plan:
    def __init__(self, pops, grps, width):
        self.pops, self.grps, self.width = pops, grps, width
        self.side = grps // 2
        self.rows = width // pops
        self.cols = width // grps
        pop_dims = [("pop", m) for m in bits_of(pops)]
        grp_dims = [("grp", 2 * m) for m in bits_of(self.side)]
        dims = []
        for k in range(max(len(pop_dims), len(grp_dims))):
            dims += pop_dims[k : k + 1] + grp_dims[k : k + 1]
        other = list(dims)
        for k in range(0, len(dims) - 1, 2):
            other[k], other[k + 1] = dims[k + 1], dims[k]
        self.orders = (dims, other)
        self.phases = len(dims)
        self.blocks = 1 << self.phases
        self.masks = [[self.mask(order, p) for p in range(self.blocks)] for order in self.orders]
        last = max([k for order in self.orders for k, (axis, m) in enumerate(order) if axis == "grp"], default=-1)
        self.run = 1 << (self.phases - 1 - last)
        self.chunks = []
        size = self.blocks
        while size > 1:
            size //= 2
            self.chunks.append([(size + size // 2, 2 * size), (size, size + size // 2)] if size > 1 else [(1, 2)])
        self.chunks.append([(0, 1)])

    def mask(self, order, p):
        pop = grp = 0
        for k, (axis, m) in enumerate(order):
            if p >> (len(order) - 1 - k) & 1:
                pop, grp = (pop ^ m, grp) if axis == "pop" else (pop, grp ^ m)
        return pop * self.side + grp // 2

    def pairs(self, of):
        out = []
        for p in range(self.pops):
            for g in range(self.grps):
                axis, m = of[g & 1]
                q, h = (p ^ m, g) if axis == "pop" else (p, g ^ m)
                out.append((p * self.grps + g, q * self.grps + h))
        return out


def moment_into(plan, place_ref, other, at_ref, a_ref, ranges, out_refs):
    rows, cols, side, run = plan.rows, plan.cols, plan.side, plan.run
    here = place_ref[0] * side + place_ref[1] // 2
    color = lax.rem(place_ref[1] + other, 2)
    where = {}
    for (lo, hi), ref in zip(ranges, out_refs, strict=True):
        for p in range(lo, hi):
            where[p] = (ref, (p - lo) * rows)
    for first in range(0, plan.blocks, run):
        if first not in where:
            continue
        places = [here ^ jnp.where(color == 0, plan.masks[0][first + k], plan.masks[1][first + k]) for k in range(run)]
        parts = [at_ref[pl.ds(pl.multiple_of(b // side * rows, rows), rows), :] for b in places]
        lhs = jnp.concatenate(parts, axis=0) if run > 1 else parts[0]
        chunk = color * side + lax.rem(places[0], side)
        rhs = a_ref[:, pl.ds(pl.multiple_of(chunk * cols, cols), cols)]
        got = jnp.dot(lhs, rhs, preferred_element_type=jnp.float32)
        for k in range(run):
            ref, at = where[first + k]
            ref[pl.ds(at, rows), :] = got[k * rows : (k + 1) * rows]


def first_kernel(plan, ranges, cuts, place_ref, w_hbm, a_hbm, a_ref, at_ref, sums_ref, *refs):
    out_refs, (w_ref, sems) = refs[:-2], refs[-2:]
    height = a_ref.shape[0] // cuts
    copies = [pltpu.make_async_copy(w_hbm, w_ref, sems.at[cuts])]
    for k in range(cuts):
        sl = pl.ds(k * height, height)
        copies.append(pltpu.make_async_copy(a_hbm.at[sl, :], a_ref.at[sl, :], sems.at[k]))
    for copy in copies:
        copy.start()
    copies[0].wait()
    w = w_ref[...].astype(jnp.float32)
    wide = w.astype(jnp.bfloat16)
    for k in range(cuts):
        copies[k + 1].wait()
        sl = pl.ds(k * height, height)
        for c in range(plan.width // 128):
            turned = jnp.transpose(a_ref[sl, c * 128 : (c + 1) * 128])
            at_ref[pl.ds(c * 128, 128), sl] = turned * wide[:, k * height : (k + 1) * height]
    moment_into(plan, place_ref, 1, at_ref, a_ref, ranges, out_refs)
    tall = jnp.broadcast_to(w, (16, w.shape[1])).astype(jnp.bfloat16)
    sums = jnp.dot(tall, a_ref[...], preferred_element_type=jnp.float32)
    lines = plan.width // 128
    for k in range(lines):
        sums_ref[pl.ds(k, 1), :] = sums[0:1, k * 128 : (k + 1) * 128]
    total = jnp.sum(w, axis=1, keepdims=True)
    sums_ref[pl.ds(lines, 8), :] = jnp.broadcast_to(total, (8, 128))


def f32(*shape):
    return jax.ShapeDtypeStruct(shape, jnp.float32)


def first(plan, place, weight, actions, ranges):
    count, width = actions.shape
    cuts = max(1, min(4, count // 128))
    held = jax.ShapeDtypeStruct((count, width), jnp.bfloat16)
    turned = jax.ShapeDtypeStruct((width, count), jnp.bfloat16)
    outs = [held, turned, f32(width // 128 + 8, 128)] + [f32((hi - lo) * plan.rows, plan.cols) for lo, hi in ranges]
    return pl.pallas_call(
        functools.partial(first_kernel, plan, ranges, cuts),
        out_shape=outs,
        in_specs=[SMEM, HBM, HBM],
        out_specs=[VMEM] * len(outs),
        scratch_shapes=[pltpu.VMEM((1, count), jnp.int32), pltpu.SemaphoreType.DMA((cuts + 1,))],
        compiler_params=pltpu.CompilerParams(vmem_limit_bytes=16 << 20),
        cost_estimate=pl.CostEstimate(flops=1 << 29, bytes_accessed=4 << 20, transcendentals=0),
        name="first",
    )(place, pltpu.with_memory_space_constraint(weight, pltpu.HBM), pltpu.with_memory_space_constraint(actions, pltpu.HBM))


def second_kernel(plan, theirs, ours, place_ref, at_ref, a_ref, *refs):
    moment_into(plan, place_ref, 1, at_ref, a_ref, theirs, refs[: len(theirs)])
    moment_into(plan, place_ref, 0, at_ref, a_ref, ours, refs[len(theirs) :])


def second(plan, place, at, actions, theirs, ours):
    outs = [f32((hi - lo) * plan.rows, plan.cols) for lo, hi in theirs + ours]
    got = pl.pallas_call(
        functools.partial(second_kernel, plan, theirs, ours),
        out_shape=outs,
        in_specs=[SMEM, VMEM, VMEM],
        out_specs=[VMEM] * len(outs),
        compiler_params=pltpu.CompilerParams(vmem_limit_bytes=16 << 20),
        cost_estimate=pl.CostEstimate(flops=3 << 29, bytes_accessed=6 << 20, transcendentals=0),
        name="second",
    )(place, at, actions)
    return got[: len(theirs)], got[len(theirs) :]


def rollout_kernel(act, first, steps, scale, fresh, a_ref, ws_ref, wa_ref, b_ref, wo_ref, r_ref, *refs):
    per = 128 // act
    if fresh:
        s0_ref, out_refs = refs[0], refs[1:]
        rows = a_ref.shape[0]
        state = jnp.broadcast_to(s0_ref[...], (rows, s0_ref.shape[1]))
        total = jnp.zeros(state.shape, jnp.float32)
    else:
        out_refs = refs[2:]
        state, total = refs[0][...], refs[1][...]
    st_ref, sum_ref = out_refs[-2:]
    st_ref[...] = state
    sum_ref[...] = total

    def body(k, unused):
        off = pl.multiple_of(k * 128, 128)
        for j in range(per):
            st = st_ref[...]
            pre = jnp.dot(st.astype(jnp.bfloat16), ws_ref[...], preferred_element_type=jnp.float32)
            pre = pre + jnp.dot(a_ref[:, pl.ds(off, 128)], wa_ref[j], preferred_element_type=jnp.float32)
            hid = jnp.tanh(pre + b_ref[...]).astype(jnp.bfloat16)
            st = 0.9 * st + jnp.dot(hid, wo_ref[...], preferred_element_type=jnp.float32)
            st_ref[...] = st
            sum_ref[...] += st
        return unused

    lax.fori_loop(first // per, (first + steps) // per, body, 0)
    if scale is not None:
        weighted = sum_ref[...] * r_ref[...]
        ones = jnp.ones((8, weighted.shape[1]), jnp.float32)
        line = lax.dot_general(ones, weighted, (((1,), (1,)), ((), ())), precision=lax.Precision.HIGHEST)
        out_refs[0][...] = line[0:1] / scale


def rollout(carry, first, steps, scale, act, actions, init_state, w_state, wide_action, bias, w_out, reward_vec):
    rows, width = actions.shape[0], init_state.shape[1]
    hidden = w_out.shape[0]
    operands = [actions, w_state, wide_action, bias, w_out, reward_vec]
    operands += [init_state] if carry is None else list(carry)
    last = scale is not None
    flops = 2 * rows * steps * (2 * width * hidden + 128 * hidden)
    return pl.pallas_call(
        functools.partial(rollout_kernel, act, first, steps, scale, carry is None),
        out_shape=f32(1, rows) if last else (f32(rows, width), f32(rows, width)),
        in_specs=[VMEM] * len(operands),
        out_specs=VMEM if last else (VMEM, VMEM),
        scratch_shapes=[pltpu.VMEM((rows, width), jnp.float32)] * (2 if last else 0),
        compiler_params=pltpu.CompilerParams(vmem_limit_bytes=16 << 20),
        cost_estimate=pl.CostEstimate(flops=flops, bytes_accessed=1 << 20, transcendentals=rows * steps * hidden),
        name="rollout",
    )(*operands)


def finish_kernel(plan, place_ref, sums_ref, *refs):
    pieces, (mean_ref, cov_ref) = refs[:-2], refs[-2:]
    rows, cols, side, width = plan.rows, plan.cols, plan.side, plan.width
    lines = width // 128
    count = sums_ref[pl.ds(lines, 1), :]
    inverse = 1.0 / count[:, 0:1]
    means = sums_ref[pl.ds(0, lines), :] / count
    mean_ref[...] = jnp.concatenate([means[k : k + 1] for k in range(lines)], axis=1)
    pop, grp = place_ref[0], place_ref[1]
    line, inner = pop * rows // 128, lax.rem(pop * rows, 128)
    mine = sums_ref[pl.ds(line, 1), :] / count
    column = jnp.transpose(jnp.broadcast_to(mine, (128, 128)))
    if rows < 128:
        choice = jnp.zeros((rows, 128), jnp.float32)
        for k in range(128 // rows):
            choice = jnp.where(inner == k * rows, column[k * rows : (k + 1) * rows], choice)
        column = choice
    left = jnp.concatenate([column] * (cols // 128), axis=1)
    for k, piece in enumerate(pieces):
        color, y = k // side, k % side
        at = (lax.rem(grp, 2) ^ color) * side + ((grp // 2) ^ y)
        sl = pl.ds(pl.multiple_of(at * cols, cols), cols)
        cov_ref[:, sl] = piece[...] * inverse - left * mean_ref[:, sl]


def finish(plan, place, sums, pieces):
    return pl.pallas_call(
        functools.partial(finish_kernel, plan),
        out_shape=(f32(1, plan.width), f32(plan.rows, plan.width)),
        in_specs=[SMEM] + [VMEM] * (1 + len(pieces)),
        out_specs=(VMEM, VMEM),
        compiler_params=pltpu.CompilerParams(vmem_limit_bytes=8 << 20),
        name="finish",
    )(place, sums, *pieces)


def on_device(plan, actions, elite_mask, init_state, w_state, w_action, bias, w_out, reward_vec):
    act = w_action.shape[0]
    steps = actions.shape[1] // act
    rows, phases, chunks = plan.rows, plan.phases, plan.chunks
    place = jnp.stack([lax.axis_index("pop"), lax.axis_index("grp")]).astype(jnp.int32)

    def send(x, of):
        return lax.ppermute(x, ALL, plan.pairs(of))

    rest = [(0, plan.blocks // 2)]
    ours = [r for level in chunks for r in level]
    actions, at, sums, *outs = first(plan, place, elite_mask[None, :], actions, chunks[0])
    got = [(r, send(x, CORE)) for r, x in zip(chunks[0], outs, strict=True)]
    sums = sums + send(sums, CORE)
    theirs, own = second(plan, place, at, actions, rest, ours)
    got.append((rest[0], send(theirs[0], CORE)))
    own = dict(zip(ours, own, strict=True))

    def total(lo, hi):
        out = own[lo, hi]
        for (a, b), x in got:
            if a <= lo and hi <= b:
                out = out + x[(lo - a) * rows : (hi - a) * rows]
        return out

    per = 128 // act
    wide_action = jnp.stack([jnp.pad(w_action, ((j * act, 128 - (j + 1) * act), (0, 0))) for j in range(per)])
    fixed = (act, actions, init_state[None, :], w_state, wide_action, bias[None, :], w_out, reward_vec[None, :])
    done, carry = 0, None
    for i, piece in enumerate(PIECES):
        last = i == len(PIECES) - 1
        piece = steps - done if last else piece * steps // sum(PIECES) // per * per
        carry = rollout(carry, done, piece, steps if last else None, *fixed)
        done += piece
    returns = carry[0]

    for k in range(phases):
        of = (plan.orders[0][k], plan.orders[1][k])
        sums = sums + send(sums, of)
        for lo, hi in chunks[k]:
            x = total(lo, hi)
            base = 0 if hi - lo == 1 << (phases - 1 - k) else lo - (1 << (phases - 1 - k))
            got.append(((base, base + hi - lo), send(x, of)))
    pieces = [total(0, 1)]
    for m in bits_of(plan.side):
        pieces += [send(x, (("grp", 2 * m), ("grp", 2 * m))) for x in pieces]
    pieces += [send(x, CORE) for x in pieces]
    new_mean, covariance = finish(plan, place, sums, pieces)
    return (new_mean[0], covariance, returns)


def solution(mesh):
    placed = (P(ALL, None), P(ALL), P(), P(), P(), P(), P(), P())
    pops, grps = mesh.shape["pop"], mesh.shape["grp"]

    def run(actions, *rest):
        plan = Plan(pops, grps, actions.shape[1])

        def body(*args):
            return on_device(plan, *args)

        return jax.shard_map(
            body, mesh=mesh, in_specs=placed, out_specs=(P(), P("pop", None), P(ALL)), check_vma=False
        )(actions, *rest)

    return run
```

profile of v0, /device:TPU:0, one launch (start us, length us, event | category | flops | bytes accessed | tf_op | source)
XLA Modules:
  0.0 62.3 jit_solution(12194141559662605447)
XLA Ops:
  0.7 2.6 %first.1 = (bf16[512,1024]{1,0:T(8,128)(2,1)S(1)}, bf16[1024,512]{1,0:T(8,128)(2,1)S(1)}, f32[16,128]{1,0:T(8,128)S(1)}, f32[512,256]{1,0:T(8,128)S(1)}, f32[512,256]{1,0:T(8,128)S(1)}) custom-call(s32[2]{0:T(128)S(1)} %pad_add_fusion.place_ref, s32[1,512]{1,0:T(1,128)} %bitcast.35, bf16[512,1024]{1,0:T(8,128)(2,1)} %a_hbm.1), custom_call_target="tpu_custom_call" | custom-call | flops 536870912 | bytes 4194304 | tf_op jit(solution)/shard_map/first/pallas_call | solution.py:126
  3.3 0.6 collective-permute-start.8
  3.8 1.6 %second.1 = (f32[1024,256]{1,0:T(8,128)S(1)}, f32[512,256]{1,0:T(8,128)S(1)}, f32[512,256]{1,0:T(8,128)S(1)}, f32[256,256]{1,0:T(8,128)S(1)}, f32[256,256]{1,0:T...) custom-call(s32[2]{0:T(128)S(1)} %pad_add_fusion.place_ref, ...), custom_call_target="tpu_custom_call" | custom-call | flops 1610612736 | bytes 6291456 | tf_op jit(solution)/shard_map/second/pallas_call | solution.py:145
  5.5 0.5 collective-permute-start.6
  6.1 2.6 %collective-permute-start.9 = (f32[512,256]{1,0:T(8,128)S(1)}, f32[512,256]{1,0:T(8,128)S(1)}, u32[]{:S(2)}, u32[]{:S(2)}) collective-permute-start(f32[512,256]{1,0:T(8,128)S(1)} %add.95), channel_id=1, source_target_pairs={{0,4},{1,3},{2,6},{3,1},{4,0},{5,7},{6,2},{7,5},{8,12},{9,11},{10,... | collective-permute-start | bytes 1572872 | tf_op jit(solution)/shard_map/ppermute | solution.py:253
  9.0 2.7 %collective-permute-start.7 = (f32[512,256]{1,0:T(8,128)S(1)}, f32[512,256]{1,0:T(8,128)S(1)}, u32[]{:S(2)}, u32[]{:S(2)}) collective-permute-start(f32[512,256]{1,0:T(8,128)S(1)} %add.92), channel_id=1, source_target_pairs={{0,4},{1,3},{2,6},{3,1},{4,0},{5,7},{6,2},{7,5},{8,12},{9,11},{10,... | collective-permute-start | bytes 1572872 | tf_op jit(solution)/shard_map/ppermute | solution.py:253
  11.6 4.2 %collective-permute-done.9 = f32[512,256]{1,0:T(8,128)S(1)} collective-permute-done((f32[512,256]{1,0:T(8,128)S(1)}, f32[512,256]{1,0:T(8,128)S(1)}, u32[]{:S(2)}, u32[]{:S(2)}) %collective-permute-start.9) | collective-permute-done | bytes 524320 | tf_op jit(solution)/shard_map/ppermute | solution.py:253
  16.0 2.1 %collective-permute-start.11 = (f32[256,256]{1,0:T(8,128)S(1)}, f32[256,256]{1,0:T(8,128)S(1)}, u32[]{:S(2)}, u32[]{:S(2)}) collective-permute-start(f32[256,256]{1,0:T(8,128)S(1)} %get-tuple-element.66), channel_id=1, source_target_pairs={{0,2},{1,5},{2,0},{3,7},{4,6},{5,1},{6,4},{7,3},{8,10},{9,13},{10,... | collective-permute-start | bytes 786440 | tf_op jit(solution)/shard_map/ppermute | solution.py:253
  18.2 6.2 %collective-permute-done.7 = f32[512,256]{1,0:T(8,128)S(1)} collective-permute-done((f32[512,256]{1,0:T(8,128)S(1)}, f32[512,256]{1,0:T(8,128)S(1)}, u32[]{:S(2)}, u32[]{:S(2)}) %collective-permute-start.7) | collective-permute-done | bytes 524320 | tf_op jit(solution)/shard_map/ppermute | solution.py:253
  24.5 2.5 %collective-permute-start.13 = (f32[128,256]{1,0:T(8,128)S(1)}, f32[128,256]{1,0:T(8,128)S(1)}, u32[]{:S(2)}, u32[]{:S(2)}) collective-permute-start(f32[128,256]{1,0:T(8,128)S(1)} %get-tuple-element.64), channel_id=1, source_target_pairs={{0,8},{1,17},{2,10},{3,19},{4,12},{5,21},{6,14},{7,23},{8,0},{9,25... | collective-permute-start | bytes 393224 | tf_op jit(solution)/shard_map/ppermute | solution.py:253
  27.0 1.6 %collective-permute-start.12 = (f32[128,256]{1,0:T(8,128)S(1)}, f32[128,256]{1,0:T(8,128)S(1)}, u32[]{:S(2)}, u32[]{:S(2)}) collective-permute-start(f32[128,256]{1,0:T(8,128)S(1)} %get-tuple-element.63), channel_id=1, source_target_pairs={{0,8},{1,17},{2,10},{3,19},{4,12},{5,21},{6,14},{7,23},{8,0},{9,25... | collective-permute-start | bytes 393224 | tf_op jit(solution)/shard_map/ppermute | solution.py:253
  28.6 2.0 %collective-permute-done.13 = f32[128,256]{1,0:T(8,128)S(1)} collective-permute-done((f32[128,256]{1,0:T(8,128)S(1)}, f32[128,256]{1,0:T(8,128)S(1)}, u32[]{:S(2)}, u32[]{:S(2)}) %collective-permute-start.13) | collective-permute-done | bytes 131104 | tf_op jit(solution)/shard_map/ppermute | solution.py:253
  30.7 3.6 %collective-permute-start.14 = (f32[128,256]{1,0:T(8,128)S(1)}, f32[128,256]{1,0:T(8,128)S(1)}, u32[]{:S(2)}, u32[]{:S(2)}) collective-permute-start(f32[128,256]{1,0:T(8,128)S(1)} %fusion), channel_id=1, source_target_pairs={{0,16},{1,9},{2,18},{3,11},{4,20},{5,13},{6,22},{7,15},{8,24},{9,1... | collective-permute-start | bytes 393224 | tf_op jit(solution)/shard_map/ppermute | solution.py:253
  34.4 0.8 %copy-done = bf16[256,256]{1,0:T(8,128)(2,1)S(1)} copy-done((bf16[256,256]{1,0:T(8,128)(2,1)S(1)}, bf16[256,256]{1,0:T(8,128)(2,1)}, u32[]{:S(2)}) %copy-start) | copy-done | bytes 131096
  35.3 1.8 %rollout.8 = (f32[512,256]{1,0:T(8,128)S(1)}, f32[512,256]{1,0:T(8,128)S(1)}) custom-call(bf16[512,1024]{1,0:T(8,128)(2,1)S(1)} %get-tuple-element.35.a_ref, bf16[256,256]{1,0:T(8,128)(2,1)S(1)} %copy-done, bf16[4,128,256]{2,1,0:T(8,128)(2,1)S(1)} %pad_maximum_fusion.wa_ref, f32[1,256]{1,0:T(1,128)S(1)} %bitcast.16, bf16[256,256]{1,0:T(8,128)(2,1)S(1)} %copy-done.1, ...), custom_call_target="tpu_custom_call" | custom-call | flops 671088640 | bytes 1048576 | tf_op jit(solution)/shard_map/rollout/pallas_call | solution.py:198
  37.0 1.8 %rollout.9 = (f32[512,256]{1,0:T(8,128)S(1)}, f32[512,256]{1,0:T(8,128)S(1)}) custom-call(bf16[512,1024]{1,0:T(8,128)(2,1)S(1)} %get-tuple-element.35.a_ref, bf16[256,256]{1,0:T(8,128)(2,1)S(1)} %copy-done, bf16[4,128,256]{2,1,0:T(8,128)(2,1)S(1)} %pad_maximum_fusion.wa_ref, f32[1,256]{1,0:T(1,128)S(1)} %bitcast.17, bf16[256,256]{1,0:T(8,128)(2,1)S(1)} %copy-done.1, ...), custom_call_target="tpu_custom_call" | custom-call | flops 671088640 | bytes 1048576 | tf_op jit(solution)/shard_map/rollout/pallas_call | solution.py:198
  38.9 1.6 %collective-permute-start.15 = (f32[128,256]{1,0:T(8,128)S(1)}, f32[128,256]{1,0:T(8,128)S(1)}, u32[]{:S(2)}, u32[]{:S(2)}) collective-permute-start(f32[128,256]{1,0:T(8,128)S(1)} %fusion.2.refs_0_), channel_id=1, source_target_pairs={{0,2},{1,3},{2,0},{3,1},{4,6},{5,7},{6,4},{7,5},{8,10},{9,11},{10,... | collective-permute-start | bytes 393224 | tf_op jit(solution)/shard_map/ppermute | solution.py:253
  40.5 1.8 %rollout.10 = (f32[512,256]{1,0:T(8,128)S(1)}, f32[512,256]{1,0:T(8,128)S(1)}) custom-call(bf16[512,1024]{1,0:T(8,128)(2,1)S(1)} %get-tuple-element.35.a_ref, bf16[256,256]{1,0:T(8,128)(2,1)S(1)} %copy-done, bf16[4,128,256]{2,1,0:T(8,128)(2,1)S(1)} %pad_maximum_fusion.wa_ref, f32[1,256]{1,0:T(1,128)S(1)} %bitcast.18, bf16[256,256]{1,0:T(8,128)(2,1)S(1)} %copy-done.1, ...), custom_call_target="tpu_custom_call" | custom-call | flops 671088640 | bytes 1048576 | tf_op jit(solution)/shard_map/rollout/pallas_call | solution.py:198
  42.3 1.8 %rollout.11 = (f32[512,256]{1,0:T(8,128)S(1)}, f32[512,256]{1,0:T(8,128)S(1)}) custom-call(bf16[512,1024]{1,0:T(8,128)(2,1)S(1)} %get-tuple-element.35.a_ref, bf16[256,256]{1,0:T(8,128)(2,1)S(1)} %copy-done, bf16[4,128,256]{2,1,0:T(8,128)(2,1)S(1)} %pad_maximum_fusion.wa_ref, f32[1,256]{1,0:T(1,128)S(1)} %bitcast.19, bf16[256,256]{1,0:T(8,128)(2,1)S(1)} %copy-done.1, ...), custom_call_target="tpu_custom_call" | custom-call | flops 671088640 | bytes 1048576 | tf_op jit(solution)/shard_map/rollout/pallas_call | solution.py:198
  44.1 1.6 %collective-permute-start.1 = (f32[16,128]{1,0:T(8,128)S(1)}, f32[16,128]{1,0:T(8,128)S(1)}, u32[]{:S(2)}, u32[]{:S(2)}) collective-permute-start(f32[16,128]{1,0:T(8,128)S(1)} %add.86), channel_id=1, source_target_pairs={{0,4},{1,3},{2,6},{3,1},{4,0},{5,7},{6,2},{7,5},{8,12},{9,11},{10,... | collective-permute-start | bytes 24584 | tf_op jit(solution)/shard_map/ppermute | solution.py:253
  45.7 1.8 %rollout.12 = (f32[512,256]{1,0:T(8,128)S(1)}, f32[512,256]{1,0:T(8,128)S(1)}) custom-call(bf16[512,1024]{1,0:T(8,128)(2,1)S(1)} %get-tuple-element.35.a_ref, bf16[256,256]{1,0:T(8,128)(2,1)S(1)} %copy-done, bf16[4,128,256]{2,1,0:T(8,128)(2,1)S(1)} %pad_maximum_fusion.wa_ref, f32[1,256]{1,0:T(1,128)S(1)} %bitcast.20, bf16[256,256]{1,0:T(8,128)(2,1)S(1)} %copy-done.1, ...), custom_call_target="tpu_custom_call" | custom-call | flops 671088640 | bytes 1048576 | tf_op jit(solution)/shard_map/rollout/pallas_call | solution.py:198
  47.5 0.4 collective-permute-done.1
  47.9 0.5 collective-permute-start.2
  48.4 0.5 collective-permute-start.17
  48.9 1.8 %rollout.13 = (f32[512,256]{1,0:T(8,128)S(1)}, f32[512,256]{1,0:T(8,128)S(1)}) custom-call(bf16[512,1024]{1,0:T(8,128)(2,1)S(1)} %get-tuple-element.35.a_ref, bf16[256,256]{1,0:T(8,128)(2,1)S(1)} %copy-done, bf16[4,128,256]{2,1,0:T(8,128)(2,1)S(1)} %pad_maximum_fusion.wa_ref, f32[1,256]{1,0:T(1,128)S(1)} %bitcast.21, bf16[256,256]{1,0:T(8,128)(2,1)S(1)} %copy-done.1, ...), custom_call_target="tpu_custom_call" | custom-call | flops 671088640 | bytes 1048576 | tf_op jit(solution)/shard_map/rollout/pallas_call | solution.py:198
  50.6 0.9 %collective-permute-done.2 = f32[16,128]{1,0:T(8,128)S(1)} collective-permute-done((f32[16,128]{1,0:T(8,128)S(1)}, f32[16,128]{1,0:T(8,128)S(1)}, u32[]{:S(2)}, u32[]{:S(2)}) %collective-permute-start.2) | collective-permute-done | bytes 8224 | tf_op jit(solution)/shard_map/ppermute | solution.py:253
  51.5 2.6 %collective-permute-start.3 = (f32[16,128]{1,0:T(8,128)S(1)}, f32[16,128]{1,0:T(8,128)S(1)}, u32[]{:S(2)}, u32[]{:S(2)}) collective-permute-start(f32[16,128]{1,0:T(8,128)S(1)} %add.88), channel_id=1, source_target_pairs={{0,8},{1,17},{2,10},{3,19},{4,12},{5,21},{6,14},{7,23},{8,0},{9,25... | collective-permute-start | bytes 24584 | tf_op jit(solution)/shard_map/ppermute | solution.py:253
  54.1 2.0 %rollout.14 = (f32[512,256]{1,0:T(8,128)S(1)}, f32[512,256]{1,0:T(8,128)S(1)}) custom-call(bf16[512,1024]{1,0:T(8,128)(2,1)S(1)} %get-tuple-element.35.a_ref, bf16[256,256]{1,0:T(8,128)(2,1)S(1)} %copy-done, bf16[4,128,256]{2,1,0:T(8,128)(2,1)S(1)} %pad_maximum_fusion.wa_ref, f32[1,256]{1,0:T(1,128)S(1)} %bitcast.22, bf16[256,256]{1,0:T(8,128)(2,1)S(1)} %copy-done.1, ...), custom_call_target="tpu_custom_call" | custom-call | flops 671088640 | bytes 1048576 | tf_op jit(solution)/shard_map/rollout/pallas_call | solution.py:198
  56.1 1.6 %collective-permute-start.4 = (f32[16,128]{1,0:T(8,128)S(1)}, f32[16,128]{1,0:T(8,128)S(1)}, u32[]{:S(2)}, u32[]{:S(2)}) collective-permute-start(f32[16,128]{1,0:T(8,128)S(1)} %add.89), channel_id=1, source_target_pairs={{0,16},{1,9},{2,18},{3,11},{4,20},{5,13},{6,22},{7,15},{8,24},{9,1... | collective-permute-start | bytes 24584 | tf_op jit(solution)/shard_map/ppermute | solution.py:253
  57.7 2.8 %rollout.15 = f32[1,512]{1,0:T(1,128)} custom-call(bf16[512,1024]{1,0:T(8,128)(2,1)S(1)} %get-tuple-element.35.a_ref, bf16[256,256]{1,0:T(8,128)(2,1)S(1)} %copy-done, bf16[4,128,256]{2,1,0:T(8,128)(2,1)S(1)} %pad_maximum_fusion.wa_ref, f32[1,256]{1,0:T(1,128)S(1)} %bitcast.23, bf16[256,256]{1,0:T(8,128)(2,1)S(1)} %copy-done.1, f32[1,256]{1,0:T(1,128)S(1)} %bitcast.31, ...), custom_call_target="tpu_custom_call" | custom-call | flops 671088640 | bytes 1048576 | tf_op jit(solution)/shard_map/rollout/pallas_call | solution.py:198
  60.5 0.2 collective-permute-done.4
  60.8 1.5 %finish.1 = (f32[1,1024]{1,0:T(1,128)}, f32[128,1024]{1,0:T(8,128)}) custom-call(s32[2]{0:T(128)S(1)} %pad_add_fusion.place_ref, f32[16,128]{1,0:T(8,128)S(1)} %add.90.sums_ref, f32[128,256]{1,0:T(8,128)S(1)} %fusion.2.refs_0_, f32[128,256]{1,0:T(8,128)S(1)} %collective-permute-done.15.refs_1_, f32[128,256]{1,0:T(8,128)S(1)} %collective-permute-done.16.refs_2_, ...), custom_call_target="tpu_custom_call" | custom-call | tf_op jit(solution)/shard_map/finish/pallas_call | solution.py:236
  (41 shorter events, 1.1 us)
Async XLA Ops:
  3.3 2.7 %collective-permute-start.8 = (f32[512,256]{1,0:T(8,128)S(1)}, f32[512,256]{1,0:T(8,128)S(1)}, u32[]{:S(2)}, u32[]{:S(2)}) collective-permute-start(f32[512,256]{1,0:T(8,128)S(1)} %get-tuple-element.42), channel_id=1, source_target_pairs={{0,1},{1,0},{2,3},{3,2},{4,5},{5,4},{6,7},{7,6},{8,9},{9,8},{10,11... | collective-permute-start | bytes 1572872 | tf_op jit(solution)/shard_map/ppermute | solution.py:253
  5.4 10.4 %collective-permute-start.5 = (f32[1024,256]{1,0:T(8,128)S(1)}, f32[1024,256]{1,0:T(8,128)S(1)}, u32[]{:S(2)}, u32[]{:S(2)}) collective-permute-start(f32[1024,256]{1,0:T(8,128)S(1)} %get-tuple-element.37), channel_id=1, source_target_pairs={{0,1},{1,0},{2,3},{3,2},{4,5},{5,4},{6,7},{7,6},{8,9},{9,8},{10,11... | collective-permute-start | bytes 3145736 | tf_op jit(solution)/shard_map/ppermute | solution.py:253
  5.5 3.4 %collective-permute-start.6 = (f32[512,256]{1,0:T(8,128)S(1)}, f32[512,256]{1,0:T(8,128)S(1)}, u32[]{:S(2)}, u32[]{:S(2)}) collective-permute-start(f32[512,256]{1,0:T(8,128)S(1)} %get-tuple-element.39), channel_id=1, source_target_pairs={{0,1},{1,0},{2,3},{3,2},{4,5},{5,4},{6,7},{7,6},{8,9},{9,8},{10,11... | collective-permute-start | bytes 1572872 | tf_op jit(solution)/shard_map/ppermute | solution.py:253
  6.1 9.8 %collective-permute-start.9 = (f32[512,256]{1,0:T(8,128)S(1)}, f32[512,256]{1,0:T(8,128)S(1)}, u32[]{:S(2)}, u32[]{:S(2)}) collective-permute-start(f32[512,256]{1,0:T(8,128)S(1)} %add.95), channel_id=1, source_target_pairs={{0,4},{1,3},{2,6},{3,1},{4,0},{5,7},{6,2},{7,5},{8,12},{9,11},{10,... | collective-permute-start | bytes 1572872 | tf_op jit(solution)/shard_map/ppermute | solution.py:253
  9.0 15.4 %collective-permute-start.7 = (f32[512,256]{1,0:T(8,128)S(1)}, f32[512,256]{1,0:T(8,128)S(1)}, u32[]{:S(2)}, u32[]{:S(2)}) collective-permute-start(f32[512,256]{1,0:T(8,128)S(1)} %add.92), channel_id=1, source_target_pairs={{0,4},{1,3},{2,6},{3,1},{4,0},{5,7},{6,2},{7,5},{8,12},{9,11},{10,... | collective-permute-start | bytes 1572872 | tf_op jit(solution)/shard_map/ppermute | solution.py:253
  16.0 8.4 %collective-permute-start.11 = (f32[256,256]{1,0:T(8,128)S(1)}, f32[256,256]{1,0:T(8,128)S(1)}, u32[]{:S(2)}, u32[]{:S(2)}) collective-permute-start(f32[256,256]{1,0:T(8,128)S(1)} %get-tuple-element.66), channel_id=1, source_target_pairs={{0,2},{1,5},{2,0},{3,7},{4,6},{5,1},{6,4},{7,3},{8,10},{9,13},{10,... | collective-permute-start | bytes 786440 | tf_op jit(solution)/shard_map/ppermute | solution.py:253
  18.1 10.5 %collective-permute-start.10 = (f32[256,256]{1,0:T(8,128)S(1)}, f32[256,256]{1,0:T(8,128)S(1)}, u32[]{:S(2)}, u32[]{:S(2)}) collective-permute-start(f32[256,256]{1,0:T(8,128)S(1)} %get-tuple-element.65), channel_id=1, source_target_pairs={{0,2},{1,5},{2,0},{3,7},{4,6},{5,1},{6,4},{7,3},{8,10},{9,13},{10,... | collective-permute-start | bytes 786440 | tf_op jit(solution)/shard_map/ppermute | solution.py:253
  24.4 2.6 %copy-start.5 = (bf16[32,256]{1,0:T(8,128)(2,1)S(1)}, bf16[32,256]{1,0:T(8,128)(2,1)}, u32[]{:S(2)}) copy-start(bf16[32,256]{1,0:T(8,128)(2,1)} %param.12) | copy-start | bytes 49156
  24.5 6.1 %collective-permute-start.13 = (f32[128,256]{1,0:T(8,128)S(1)}, f32[128,256]{1,0:T(8,128)S(1)}, u32[]{:S(2)}, u32[]{:S(2)}) collective-permute-start(f32[128,256]{1,0:T(8,128)S(1)} %get-tuple-element.64), channel_id=1, source_target_pairs={{0,8},{1,17},{2,10},{3,19},{4,12},{5,21},{6,14},{7,23},{8,0},{9,25... | collective-permute-start | bytes 393224 | tf_op jit(solution)/shard_map/ppermute | solution.py:253
  27.0 17.2 %collective-permute-start = (f32[16,128]{1,0:T(8,128)S(1)}, f32[16,128]{1,0:T(8,128)S(1)}, u32[]{:S(2)}, u32[]{:S(2)}) collective-permute-start(f32[16,128]{1,0:T(8,128)S(1)} %get-tuple-element.33), channel_id=1, source_target_pairs={{0,1},{1,0},{2,3},{3,2},{4,5},{5,4},{6,7},{7,6},{8,9},{9,8},{10,11... | collective-permute-start | bytes 24584 | tf_op jit(solution)/shard_map/ppermute | solution.py:253
  27.0 11.9 %collective-permute-start.12 = (f32[128,256]{1,0:T(8,128)S(1)}, f32[128,256]{1,0:T(8,128)S(1)}, u32[]{:S(2)}, u32[]{:S(2)}) collective-permute-start(f32[128,256]{1,0:T(8,128)S(1)} %get-tuple-element.63), channel_id=1, source_target_pairs={{0,8},{1,17},{2,10},{3,19},{4,12},{5,21},{6,14},{7,23},{8,0},{9,25... | collective-permute-start | bytes 393224 | tf_op jit(solution)/shard_map/ppermute | solution.py:253
  30.7 8.2 %collective-permute-start.14 = (f32[128,256]{1,0:T(8,128)S(1)}, f32[128,256]{1,0:T(8,128)S(1)}, u32[]{:S(2)}, u32[]{:S(2)}) collective-permute-start(f32[128,256]{1,0:T(8,128)S(1)} %fusion), channel_id=1, source_target_pairs={{0,16},{1,9},{2,18},{3,11},{4,20},{5,13},{6,22},{7,15},{8,24},{9,1... | collective-permute-start | bytes 393224 | tf_op jit(solution)/shard_map/ppermute | solution.py:253
  34.3 0.9 %copy-start = (bf16[256,256]{1,0:T(8,128)(2,1)S(1)}, bf16[256,256]{1,0:T(8,128)(2,1)}, u32[]{:S(2)}) copy-start(bf16[256,256]{1,0:T(8,128)(2,1)} %ws_ref.15) | copy-start | bytes 393220
  34.3 1.0 %copy-start.1 = (bf16[256,256]{1,0:T(8,128)(2,1)S(1)}, bf16[256,256]{1,0:T(8,128)(2,1)}, u32[]{:S(2)}) copy-start(bf16[256,256]{1,0:T(8,128)(2,1)} %wo_ref.15) | copy-start | bytes 393220
  34.3 1.0 %copy-start.3 = (f32[256]{0:T(256)S(1)}, f32[256]{0:T(256)}, u32[]{:S(2)}) copy-start(f32[256]{0:T(256)} %param.15) | copy-start | bytes 3076
  34.3 1.0 %copy-start.4 = (f32[256]{0:T(256)S(1)}, f32[256]{0:T(256)}, u32[]{:S(2)}) copy-start(f32[256]{0:T(256)} %param.10) | copy-start | bytes 3076
  34.3 0.9 %copy-start.2 = (f32[256]{0:T(256)S(1)}, f32[256]{0:T(256)}, u32[]{:S(2)}) copy-start(f32[256]{0:T(256)} %param.13) | copy-start | bytes 3076
  38.9 9.4 %collective-permute-start.15 = (f32[128,256]{1,0:T(8,128)S(1)}, f32[128,256]{1,0:T(8,128)S(1)}, u32[]{:S(2)}, u32[]{:S(2)}) collective-permute-start(f32[128,256]{1,0:T(8,128)S(1)} %fusion.2.refs_0_), channel_id=1, source_target_pairs={{0,2},{1,3},{2,0},{3,1},{4,6},{5,7},{6,4},{7,5},{8,10},{9,11},{10,... | collective-permute-start | bytes 393224 | tf_op jit(solution)/shard_map/ppermute | solution.py:253
  44.1 3.7 %collective-permute-start.1 = (f32[16,128]{1,0:T(8,128)S(1)}, f32[16,128]{1,0:T(8,128)S(1)}, u32[]{:S(2)}, u32[]{:S(2)}) collective-permute-start(f32[16,128]{1,0:T(8,128)S(1)} %add.86), channel_id=1, source_target_pairs={{0,4},{1,3},{2,6},{3,1},{4,0},{5,7},{6,2},{7,5},{8,12},{9,11},{10,... | collective-permute-start | bytes 24584 | tf_op jit(solution)/shard_map/ppermute | solution.py:253
  47.9 3.7 %collective-permute-start.2 = (f32[16,128]{1,0:T(8,128)S(1)}, f32[16,128]{1,0:T(8,128)S(1)}, u32[]{:S(2)}, u32[]{:S(2)}) collective-permute-start(f32[16,128]{1,0:T(8,128)S(1)} %add.87), channel_id=1, source_target_pairs={{0,2},{1,5},{2,0},{3,7},{4,6},{5,1},{6,4},{7,3},{8,10},{9,13},{10,... | collective-permute-start | bytes 24584 | tf_op jit(solution)/shard_map/ppermute | solution.py:253
  48.4 12.4 %collective-permute-start.16 = (f32[128,256]{1,0:T(8,128)S(1)}, f32[128,256]{1,0:T(8,128)S(1)}, u32[]{:S(2)}, u32[]{:S(2)}) collective-permute-start(f32[128,256]{1,0:T(8,128)S(1)} %fusion.2.refs_0_), channel_id=1, source_target_pairs={{0,1},{1,0},{2,3},{3,2},{4,5},{5,4},{6,7},{7,6},{8,9},{9,8},{10,11... | collective-permute-start | bytes 393224 | tf_op jit(solution)/shard_map/ppermute | solution.py:253
  48.4 12.4 %collective-permute-start.17 = (f32[128,256]{1,0:T(8,128)S(1)}, f32[128,256]{1,0:T(8,128)S(1)}, u32[]{:S(2)}, u32[]{:S(2)}) collective-permute-start(f32[128,256]{1,0:T(8,128)S(1)} %collective-permute-done.15.refs_1_), channel_id=1, source_target_pairs={{0,1},{1,0},{2,3},{3,2},{4,5},{5,4},{6,7},{7,6},{8,9},{9,8},{10,11... | collective-permute-start | bytes 393224 | tf_op jit(solution)/shard_map/ppermute | solution.py:253
  51.5 4.6 %collective-permute-start.3 = (f32[16,128]{1,0:T(8,128)S(1)}, f32[16,128]{1,0:T(8,128)S(1)}, u32[]{:S(2)}, u32[]{:S(2)}) collective-permute-start(f32[16,128]{1,0:T(8,128)S(1)} %add.88), channel_id=1, source_target_pairs={{0,8},{1,17},{2,10},{3,19},{4,12},{5,21},{6,14},{7,23},{8,0},{9,25... | collective-permute-start | bytes 24584 | tf_op jit(solution)/shard_map/ppermute | solution.py:253
  56.1 4.6 %collective-permute-start.4 = (f32[16,128]{1,0:T(8,128)S(1)}, f32[16,128]{1,0:T(8,128)S(1)}, u32[]{:S(2)}, u32[]{:S(2)}) collective-permute-start(f32[16,128]{1,0:T(8,128)S(1)} %add.89), channel_id=1, source_target_pairs={{0,16},{1,9},{2,18},{3,11},{4,20},{5,13},{6,22},{7,15},{8,24},{9,1... | collective-permute-start | bytes 24584 | tf_op jit(solution)/shard_map/ppermute | solution.py:253
where the time goes:
time: 62.5 us; the launch traced here: 62.3 us
  starting transfers between devices  24.7 us (40%)
  Pallas kernels  21.1 us (34%)
  waiting for transfers between devices  14.2 us (23%)
  local copies, waits for them, and re-layouts  0.94 us (2%)
  between operations  0.82 us (1%)
    ppermute x18, starting transfers between devices, send(): return lax.ppermute(x, ALL, plan.pairs(of))  24.7 us
    pallas_call x8, Pallas kernels, rollout(): pl.pallas_call(functools.partial(rollout_kernel, act, first, steps, scale...  15.4 us
    ppermute x18, waiting for transfers between devices, send(): return lax.ppermute(x, ALL, plan.pairs(of))  14.2 us
    pallas_call x1, Pallas kernels, first(): pl.pallas_call(functools.partial(first_kernel, plan, ranges, cuts), out_s...  2.57 us
    pallas_call x1, Pallas kernels, second(): pl.pallas_call(functools.partial(second_kernel, plan, theirs, ours), out_...  1.55 us
    pallas_call x1, Pallas kernels, finish(): pl.pallas_call(functools.partial(finish_kernel, plan), out_shape=(f32(1,...  1.49 us
  transfers between devices with their start and end apart: 18, of which 7 were waited for; matrix products, arithmetic and copies ran while one was open for 1% of the time, Pallas kernels for 27%

commit v1 on v0

--- a/solution.py
+++ b/solution.py
@@ -25,6 +25,7 @@
         self.side = grps // 2
         self.rows = width // pops
         self.cols = width // grps
+        self.tail = (width // self.cols + 1 + 7) // 8 * 8
         pop_dims = [("pop", m) for m in bits_of(pops)]
         grp_dims = [("grp", 2 * m) for m in bits_of(self.side)]
         dims = []
@@ -85,7 +86,7 @@
             ref[pl.ds(at, rows), :] = got[k * rows : (k + 1) * rows]
 
 
-def first_kernel(plan, ranges, cuts, place_ref, w_hbm, a_hbm, a_ref, at_ref, sums_ref, *refs):
+def first_kernel(plan, ranges, cuts, place_ref, w_hbm, a_hbm, a_ref, at_ref, *refs):
     out_refs, (w_ref, sems) = refs[:-2], refs[-2:]
     height = a_ref.shape[0] // cuts
     copies = [pltpu.make_async_copy(w_hbm, w_ref, sems.at[cuts])]
@@ -106,11 +107,13 @@
     moment_into(plan, place_ref, 1, at_ref, a_ref, ranges, out_refs)
     tall = jnp.broadcast_to(w, (16, w.shape[1])).astype(jnp.bfloat16)
     sums = jnp.dot(tall, a_ref[...], preferred_element_type=jnp.float32)
-    lines = plan.width // 128
-    for k in range(lines):
-        sums_ref[pl.ds(k, 1), :] = sums[0:1, k * 128 : (k + 1) * 128]
+    lo, hi = ranges[0]
+    base, cols = (hi - lo) * plan.rows, plan.cols
+    for k in range(plan.width // cols):
+        out_refs[0][pl.ds(base + k, 1), :] = sums[0:1, k * cols : (k + 1) * cols]
+    left = plan.tail - plan.width // cols
     total = jnp.sum(w, axis=1, keepdims=True)
-    sums_ref[pl.ds(lines, 8), :] = jnp.broadcast_to(total, (8, 128))
+    out_refs[0][pl.ds(base + plan.width // cols, left), :] = jnp.broadcast_to(total, (left, cols))
 
 
 def f32(*shape):
@@ -122,7 +125,8 @@
     cuts = max(1, min(4, count // 128))
     held = jax.ShapeDtypeStruct((count, width), jnp.bfloat16)
     turned = jax.ShapeDtypeStruct((width, count), jnp.bfloat16)
-    outs = [held, turned, f32(width // 128 + 8, 128)] + [f32((hi - lo) * plan.rows, plan.cols) for lo, hi in ranges]
+    outs = [held, turned]
+    outs += [f32((hi - lo) * plan.rows + (0 if i else plan.tail), plan.cols) for i, (lo, hi) in enumerate(ranges)]
     return pl.pallas_call(
         functools.partial(first_kernel, plan, ranges, cuts),
         out_shape=outs,
@@ -135,23 +139,48 @@
     )(place, pltpu.with_memory_space_constraint(weight, pltpu.HBM), pltpu.with_memory_space_constraint(actions, pltpu.HBM))
 
 
-def second_kernel(plan, theirs, ours, place_ref, at_ref, a_ref, *refs):
+def later_kernel(plan, theirs, ours, place_ref, at_ref, a_ref, *refs):
     moment_into(plan, place_ref, 1, at_ref, a_ref, theirs, refs[: len(theirs)])
     moment_into(plan, place_ref, 0, at_ref, a_ref, ours, refs[len(theirs) :])
 
 
-def second(plan, place, at, actions, theirs, ours):
+def later(plan, place, at, actions, theirs, ours):
     outs = [f32((hi - lo) * plan.rows, plan.cols) for lo, hi in theirs + ours]
     got = pl.pallas_call(
-        functools.partial(second_kernel, plan, theirs, ours),
+        functools.partial(later_kernel, plan, theirs, ours),
         out_shape=outs,
         in_specs=[SMEM, VMEM, VMEM],
         out_specs=[VMEM] * len(outs),
         compiler_params=pltpu.CompilerParams(vmem_limit_bytes=16 << 20),
-        cost_estimate=pl.CostEstimate(flops=3 << 29, bytes_accessed=6 << 20, transcendentals=0),
-        name="second",
+        cost_estimate=pl.CostEstimate(flops=1 << 29, bytes_accessed=4 << 20, transcendentals=0),
+        name="later",
     )(place, at, actions)
     return got[: len(theirs)], got[len(theirs) :]
+
+
+def combine_kernel(size, tail, offsets, ends, *refs):
+    own_ref, out_ref = refs[0], refs[-1]
+    terms, (mine_ref, got_ref) = refs[1:-3], refs[-3:-1]
+    out = own_ref[...]
+    for ref, at in zip(terms, offsets, strict=True):
+        out = out + ref[pl.ds(at, size), :]
+    out_ref[pl.ds(0, size), :] = out
+    out_ref[pl.ds(size, tail), :] = mine_ref[pl.ds(ends[0], tail), :] + got_ref[pl.ds(ends[1], tail), :]
+
+
+def combine(plan, own, terms, mine, got):
+    size = own.shape[0]
+    ends = (mine.shape[0] - plan.tail, got.shape[0] - plan.tail)
+    operands = [own] + [x for x, _ in terms] + [mine, got]
+    return pl.pallas_call(
+        functools.partial(combine_kernel, size, plan.tail, [at for _, at in terms], ends),
+        out_shape=f32(size + plan.tail, plan.cols),
+        in_specs=[VMEM] * len(operands),
+        out_specs=VMEM,
+        compiler_params=pltpu.CompilerParams(vmem_limit_bytes=8 << 20),
+        cost_estimate=pl.CostEstimate(flops=1 << 18, bytes_accessed=1 << 18, transcendentals=0),
+        name="combine",
+    )(*operands)
 
 
 def rollout_kernel(act, first, steps, scale, fresh, a_ref, ws_ref, wa_ref, b_ref, wo_ref, r_ref, *refs):
@@ -207,23 +236,21 @@
     )(*operands)
 
 
-def finish_kernel(plan, place_ref, sums_ref, *refs):
-    pieces, (mean_ref, cov_ref) = refs[:-2], refs[-2:]
-    rows, cols, side, width = plan.rows, plan.cols, plan.side, plan.width
-    lines = width // 128
-    count = sums_ref[pl.ds(lines, 1), :]
+def finish_kernel(plan, ends, place_ref, mine_ref, got_ref, *refs):
+    pieces, (mean_ref, cov_ref, line_ref) = refs[:-3], refs[-3:]
+    rows, cols, side = plan.rows, plan.cols, plan.side
+    tail = mine_ref[pl.ds(ends[0], plan.tail), :] + got_ref[pl.ds(ends[1], plan.tail), :]
+    lines = plan.width // cols
+    count = tail[lines : lines + 1]
     inverse = 1.0 / count[:, 0:1]
-    means = sums_ref[pl.ds(0, lines), :] / count
-    mean_ref[...] = jnp.concatenate([means[k : k + 1] for k in range(lines)], axis=1)
+    for k in range(lines):
+        mean_ref[:, pl.ds(k * cols, cols)] = tail[k : k + 1] / count
     pop, grp = place_ref[0], place_ref[1]
-    line, inner = pop * rows // 128, lax.rem(pop * rows, 128)
-    mine = sums_ref[pl.ds(line, 1), :] / count
-    column = jnp.transpose(jnp.broadcast_to(mine, (128, 128)))
+    start = pl.multiple_of(pop * rows // 128 * 128, 128)
+    column = jnp.transpose(jnp.broadcast_to(mean_ref[:, pl.ds(start, 128)], (128, 128)))
     if rows < 128:
-        choice = jnp.zeros((rows, 128), jnp.float32)
-        for k in range(128 // rows):
-            choice = jnp.where(inner == k * rows, column[k * rows : (k + 1) * rows], choice)
-        column = choice
+        line_ref[...] = column
+        column = line_ref[pl.ds(pl.multiple_of(lax.rem(pop * rows, 128), rows), rows), :]
     left = jnp.concatenate([column] * (cols // 128), axis=1)
     for k, piece in enumerate(pieces):
         color, y = k // side, k % side
@@ -232,15 +259,17 @@
         cov_ref[:, sl] = piece[...] * inverse - left * mean_ref[:, sl]
 
 
-def finish(plan, place, sums, pieces):
+def finish(plan, place, mine, got, pieces):
+    ends = (mine.shape[0] - plan.tail, got.shape[0] - plan.tail)
     return pl.pallas_call(
-        functools.partial(finish_kernel, plan),
+        functools.partial(finish_kernel, plan, ends),
         out_shape=(f32(1, plan.width), f32(plan.rows, plan.width)),
-        in_specs=[SMEM] + [VMEM] * (1 + len(pieces)),
+        in_specs=[SMEM] + [VMEM] * (2 + len(pieces)),
         out_specs=(VMEM, VMEM),
+        scratch_shapes=[pltpu.VMEM((128, 128), jnp.float32)],
         compiler_params=pltpu.CompilerParams(vmem_limit_bytes=8 << 20),
         name="finish",
-    )(place, sums, *pieces)
+    )(place, mine, got, *pieces)
 
 
 def on_device(plan, actions, elite_mask, init_state, w_state, w_action, bias, w_out, reward_vec):
@@ -253,19 +282,22 @@
         return lax.ppermute(x, ALL, plan.pairs(of))
 
     rest = [(0, plan.blocks // 2)]
-    ours = [r for level in chunks for r in level]
-    actions, at, sums, *outs = first(plan, place, elite_mask[None, :], actions, chunks[0])
+    actions, at, *outs = first(plan, place, elite_mask[None, :], actions, chunks[0])
     got = [(r, send(x, CORE)) for r, x in zip(chunks[0], outs, strict=True)]
-    sums = sums + send(sums, CORE)
-    theirs, own = second(plan, place, at, actions, rest, ours)
+    payload, received = outs[0], got[0][1]
+    own = dict(zip(chunks[0], later(plan, place, at, actions, [], chunks[0])[1], strict=True))
+    ours = [r for level in chunks[1:] for r in level]
+    theirs, more = later(plan, place, at, actions, rest, ours)
     got.append((rest[0], send(theirs[0], CORE)))
-    own = dict(zip(ours, own, strict=True))
+    own.update(zip(ours, more, strict=True))
+
+    def terms(lo, hi):
+        return [(x, (lo - a) * rows) for (a, b), x in got if a <= lo and hi <= b]
 
     def total(lo, hi):
         out = own[lo, hi]
-        for (a, b), x in got:
-            if a <= lo and hi <= b:
-                out = out + x[(lo - a) * rows : (hi - a) * rows]
+        for x, at in terms(lo, hi):
+            out = out + x[at : at + out.shape[0]]
         return out
 
     per = 128 // act
@@ -281,16 +313,25 @@
 
     for k in range(phases):
         of = (plan.orders[0][k], plan.orders[1][k])
-        sums = sums + send(sums, of)
-        for lo, hi in chunks[k]:
-            x = total(lo, hi)
-            base = 0 if hi - lo == 1 << (phases - 1 - k) else lo - (1 << (phases - 1 - k))
-            got.append(((base, base + hi - lo), send(x, of)))
+        base = 1 << (phases - 1 - k)
+        sent = []
+        for i, (lo, hi) in enumerate(chunks[k]):
+            if i == 0:
+                payload = combine(plan, own[lo, hi], terms(lo, hi), payload, received)
+                x = payload
+            else:
+                x = total(lo, hi)
+            x = send(x, of)
+            if i == 0:
+                received = x
+            at = 0 if hi - lo == base else lo - base
+            sent.append(((at, at + hi - lo), x))
+        got += sent
     pieces = [total(0, 1)]
     for m in bits_of(plan.side):
         pieces += [send(x, (("grp", 2 * m), ("grp", 2 * m))) for x in pieces]
     pieces += [send(x, CORE) for x in pieces]
-    new_mean, covariance = finish(plan, place, sums, pieces)
+    new_mean, covariance = finish(plan, place, payload, received, pieces)
     return (new_mean[0], covariance, returns)
 
 

time: 62.5 us -> 55.3 us (0.88)
  starting transfers between devices: 24.7 us -> 15.5 us
  waiting for transfers between devices: 14.2 us -> 15 us
  Pallas kernels: 21.1 us -> 21.9 us
    ppermute x18 -> x13, starting transfers between devices: 24.7 us -> 15.5 us  [send(): return lax.ppermute(x, ALL, plan.pairs(of))]
    pallas_call x2 -> x7, Pallas kernels: 3.05 us -> 3.97 us  [the longest x2 2.28 us: later(): pl.pallas_call(functools.partial(later_kernel, plan, theirs, ours), out_s...]
    ppermute x18 -> x13, waiting for transfers between devices: 14.2 us -> 15 us  [send(): return lax.ppermute(x, ALL, plan.pairs(of))]
  transfers between devices with their start and end apart: 18 -> 13, of which waited for: 7 -> 3; matrix products, arithmetic and copies ran while one was open for 1% -> 0% of each run, Pallas kernels for 27% -> 32%
where the time goes in v1:
time: 55.3 us; the launch traced here: 55.1 us
  Pallas kernels  21.9 us (40%)
  starting transfers between devices  15.5 us (28%)
  waiting for transfers between devices  15 us (27%)
  local copies, waits for them, and re-layouts  1.5 us (3%)
  between operations  0.81 us (1%)
    ppermute x13, starting transfers between devices, send(): return lax.ppermute(x, ALL, plan.pairs(of))  15.5 us
    pallas_call x8, Pallas kernels, rollout(): pl.pallas_call(functools.partial(rollout_kernel, act, first, steps, scale...  15.4 us
    ppermute x13, waiting for transfers between devices, send(): return lax.ppermute(x, ALL, plan.pairs(of))  15 us
    pallas_call x1, Pallas kernels, first(): pl.pallas_call(functools.partial(first_kernel, plan, ranges, cuts), out_s...  2.57 us
    pallas_call x2, Pallas kernels, later(): pl.pallas_call(functools.partial(later_kernel, plan, theirs, ours), out_s...  2.28 us
    pallas_call x1, Pallas kernels, finish(): pl.pallas_call(functools.partial(finish_kernel, plan, ends), out_shape=(f...  1.5 us
    unnamed x12, local copies, waits for them, and re-layouts  1.48 us
  transfers between devices with their start and end apart: 13, of which 3 were waited for; matrix products, arithmetic and copies ran while one was open for 0% of the time, Pallas kernels for 32%

profile of v1, /device:TPU:0, one launch (start us, length us, event | category | flops | bytes accessed | tf_op | source)
XLA Modules:
  0.0 55.1 jit_solution(3087356658387646603)
XLA Ops:
  0.6 0.1 pad_add_fusion.place_ref
  0.7 2.6 %first.1 = (bf16[512,1024]{1,0:T(8,128)(2,1)S(1)}, bf16[1024,512]{1,0:T(8,128)(2,1)S(1)}, f32[520,256]{1,0:T(8,128)S(1)}, f32[512,256]{1,0:T(8,128)S(1)}) custom-call(s32[2]{0:T(128)S(1)} %pad_add_fusion.place_ref, s32[1,512]{1,0:T(1,128)} %bitcast.35, bf16[512,1024]{1,0:T(8,128)(2,1)} %a_hbm.1), custom_call_target="tpu_custom_call" | custom-call | flops 536870912 | bytes 4194304 | tf_op jit(solution)/shard_map/first/pallas_call | solution.py:130
  3.3 0.6 %collective-permute-start.3 = (f32[520,256]{1,0:T(8,128)S(1)}, f32[520,256]{1,0:T(8,128)S(1)}, u32[]{:S(2)}, u32[]{:S(2)}) collective-permute-start(f32[520,256]{1,0:T(8,128)S(1)} %get-tuple-element.40.refs_2_), channel_id=1, source_target_pairs={{0,1},{1,0},{2,3},{3,2},{4,5},{5,4},{6,7},{7,6},{8,9},{9,8},{10,11... | collective-permute-start | bytes 1597448 | tf_op jit(solution)/shard_map/ppermute | solution.py:282
  3.8 1.3 %later.2 = (f32[1024,256]{1,0:T(8,128)S(1)}, f32[256,256]{1,0:T(8,128)S(1)}, f32[256,256]{1,0:T(8,128)S(1)}, f32[128,256]{1,0:T(8,128)S(1)}, f32[128,256]{1,0:T(...) custom-call(s32[2]{0:T(128)S(1)} %pad_add_fusion.place_ref, bf16[1024,512]{1,0:T(8,128)(2,1)S(1)} %get-tuple-element.32.at_ref, ...), custom_call_target="tpu_custom_call" | custom-call | flops 536870912 | bytes 4194304 | tf_op jit(solution)/shard_map/later/pallas_call | solution.py:149
  5.1 0.1 collective-permute-start
  5.2 0.5 collective-permute-start.1
  5.7 1.0 %later.3 = (f32[512,256]{1,0:T(8,128)S(1)}, f32[512,256]{1,0:T(8,128)S(1)}) custom-call(s32[2]{0:T(128)S(1)} %pad_add_fusion.place_ref, bf16[1024,512]{1,0:T(8,128)(2,1)S(1)} %get-tuple-element.32.at_ref, bf16[512,1024]{1,0:T(8,128)(2,1)S(1)} %get-tuple-element.33.a_ref), custom_call_target="tpu_custom_call" | custom-call | flops 536870912 | bytes 4194304 | tf_op jit(solution)/shard_map/later/pallas_call | solution.py:149
  6.7 0.1 combine.4.refs_3_
  6.8 2.6 %collective-permute-start.4 = (f32[520,256]{1,0:T(8,128)S(1)}, f32[520,256]{1,0:T(8,128)S(1)}, u32[]{:S(2)}, u32[]{:S(2)}) collective-permute-start(f32[520,256]{1,0:T(8,128)S(1)} %combine.4.refs_3_), channel_id=1, source_target_pairs={{0,4},{1,3},{2,6},{3,1},{4,0},{5,7},{6,2},{7,5},{8,12},{9,11},{10,... | collective-permute-start | bytes 1597448 | tf_op jit(solution)/shard_map/ppermute | solution.py:282
  9.5 1.9 %collective-permute-start.2 = (f32[512,256]{1,0:T(8,128)S(1)}, f32[512,256]{1,0:T(8,128)S(1)}, u32[]{:S(2)}, u32[]{:S(2)}) collective-permute-start(f32[512,256]{1,0:T(8,128)S(1)} %add.41), channel_id=1, source_target_pairs={{0,4},{1,3},{2,6},{3,1},{4,0},{5,7},{6,2},{7,5},{8,12},{9,11},{10,... | collective-permute-start | bytes 1572872 | tf_op jit(solution)/shard_map/ppermute | solution.py:282
  11.4 5.3 %collective-permute-done.4.refs_2_.refs_4_ = f32[520,256]{1,0:T(8,128)S(1)} collective-permute-done((f32[520,256]{1,0:T(8,128)S(1)}, f32[520,256]{1,0:T(8,128)S(1)}, u32[]{:S(2)}, u32[]{:S(2)}) %collective-permute-start.4) | collective-permute-done | bytes 532512 | tf_op jit(solution)/shard_map/ppermute | solution.py:282
  16.7 2.1 %collective-permute-start.6 = (f32[264,256]{1,0:T(8,128)S(1)}, f32[264,256]{1,0:T(8,128)S(1)}, u32[]{:S(2)}, u32[]{:S(2)}) collective-permute-start(f32[264,256]{1,0:T(8,128)S(1)} %combine.5.refs_4_), channel_id=1, source_target_pairs={{0,2},{1,5},{2,0},{3,7},{4,6},{5,1},{6,4},{7,3},{8,10},{9,13},{10,... | collective-permute-start | bytes 811016 | tf_op jit(solution)/shard_map/ppermute | solution.py:282
  18.9 0.1 collective-permute-start.5
  19.0 0.6 %copy-done.5 = bf16[32,256]{1,0:T(8,128)(2,1)S(1)} copy-done((bf16[32,256]{1,0:T(8,128)(2,1)S(1)}, bf16[32,256]{1,0:T(8,128)(2,1)}, u32[]{:S(2)}) %copy-start.5) | copy-done | bytes 16408
  19.6 5.7 %collective-permute-done.2.refs_2_ = f32[512,256]{1,0:T(8,128)S(1)} collective-permute-done((f32[512,256]{1,0:T(8,128)S(1)}, f32[512,256]{1,0:T(8,128)S(1)}, u32[]{:S(2)}, u32[]{:S(2)}) %collective-permute-start.2) | collective-permute-done | bytes 524320 | tf_op jit(solution)/shard_map/ppermute | solution.py:282
  25.3 2.5 %collective-permute-start.7 = (f32[136,256]{1,0:T(8,128)S(1)}, f32[136,256]{1,0:T(8,128)S(1)}, u32[]{:S(2)}, u32[]{:S(2)}) collective-permute-start(f32[136,256]{1,0:T(8,128)S(1)} %combine.6.refs_5_), channel_id=1, source_target_pairs={{0,8},{1,17},{2,10},{3,19},{4,12},{5,21},{6,14},{7,23},{8,0},{9,25... | collective-permute-start | bytes 417800 | tf_op jit(solution)/shard_map/ppermute | solution.py:282
  27.9 0.1 collective-permute-start.9
  28.0 3.9 %collective-permute-done.7.refs_4_.refs_6_ = f32[136,256]{1,0:T(8,128)S(1)} collective-permute-done((f32[136,256]{1,0:T(8,128)S(1)}, f32[136,256]{1,0:T(8,128)S(1)}, u32[]{:S(2)}, u32[]{:S(2)}) %collective-permute-start.7) | collective-permute-done | bytes 139296 | tf_op jit(solution)/shard_map/ppermute | solution.py:282
  31.9 3.0 %collective-permute-start.8 = (f32[136,256]{1,0:T(8,128)S(1)}, f32[136,256]{1,0:T(8,128)S(1)}, u32[]{:S(2)}, u32[]{:S(2)}) collective-permute-start(f32[136,256]{1,0:T(8,128)S(1)} %combine.7.mine_ref), channel_id=1, source_target_pairs={{0,16},{1,9},{2,18},{3,11},{4,20},{5,13},{6,22},{7,15},{8,24},{9,1... | collective-permute-start | bytes 417800 | tf_op jit(solution)/shard_map/ppermute | solution.py:282
  35.0 0.8 %copy-done = bf16[256,256]{1,0:T(8,128)(2,1)S(1)} copy-done((bf16[256,256]{1,0:T(8,128)(2,1)S(1)}, bf16[256,256]{1,0:T(8,128)(2,1)}, u32[]{:S(2)}) %copy-start) | copy-done | bytes 131096
  35.9 1.7 %rollout.8 = (f32[512,256]{1,0:T(8,128)S(1)}, f32[512,256]{1,0:T(8,128)S(1)}) custom-call(bf16[512,1024]{1,0:T(8,128)(2,1)S(1)} %get-tuple-element.33.a_ref, bf16[256,256]{1,0:T(8,128)(2,1)S(1)} %copy-done, bf16[4,128,256]{2,1,0:T(8,128)(2,1)S(1)} %pad_maximum_fusion.wa_ref, f32[1,256]{1,0:T(1,128)S(1)} %bitcast.16, bf16[256,256]{1,0:T(8,128)(2,1)S(1)} %copy-done.1, ...), custom_call_target="tpu_custom_call" | custom-call | flops 671088640 | bytes 1048576 | tf_op jit(solution)/shard_map/rollout/pallas_call | solution.py:227
  37.7 1.8 %rollout.9 = (f32[512,256]{1,0:T(8,128)S(1)}, f32[512,256]{1,0:T(8,128)S(1)}) custom-call(bf16[512,1024]{1,0:T(8,128)(2,1)S(1)} %get-tuple-element.33.a_ref, bf16[256,256]{1,0:T(8,128)(2,1)S(1)} %copy-done, bf16[4,128,256]{2,1,0:T(8,128)(2,1)S(1)} %pad_maximum_fusion.wa_ref, f32[1,256]{1,0:T(1,128)S(1)} %bitcast.17, bf16[256,256]{1,0:T(8,128)(2,1)S(1)} %copy-done.1, ...), custom_call_target="tpu_custom_call" | custom-call | flops 671088640 | bytes 1048576 | tf_op jit(solution)/shard_map/rollout/pallas_call | solution.py:227
  39.5 1.6 %collective-permute-start.10 = (f32[128,256]{1,0:T(8,128)S(1)}, f32[128,256]{1,0:T(8,128)S(1)}, u32[]{:S(2)}, u32[]{:S(2)}) collective-permute-start(f32[128,256]{1,0:T(8,128)S(1)} %slice_add_fusion.2.refs_0_), channel_id=1, source_target_pairs={{0,2},{1,3},{2,0},{3,1},{4,6},{5,7},{6,4},{7,5},{8,10},{9,11},{10,... | collective-permute-start | bytes 393224 | tf_op jit(solution)/shard_map/ppermute | solution.py:282
  41.1 1.8 %rollout.10 = (f32[512,256]{1,0:T(8,128)S(1)}, f32[512,256]{1,0:T(8,128)S(1)}) custom-call(bf16[512,1024]{1,0:T(8,128)(2,1)S(1)} %get-tuple-element.33.a_ref, bf16[256,256]{1,0:T(8,128)(2,1)S(1)} %copy-done, bf16[4,128,256]{2,1,0:T(8,128)(2,1)S(1)} %pad_maximum_fusion.wa_ref, f32[1,256]{1,0:T(1,128)S(1)} %bitcast.18, bf16[256,256]{1,0:T(8,128)(2,1)S(1)} %copy-done.1, ...), custom_call_target="tpu_custom_call" | custom-call | flops 671088640 | bytes 1048576 | tf_op jit(solution)/shard_map/rollout/pallas_call | solution.py:227
  42.9 1.8 %rollout.11 = (f32[512,256]{1,0:T(8,128)S(1)}, f32[512,256]{1,0:T(8,128)S(1)}) custom-call(bf16[512,1024]{1,0:T(8,128)(2,1)S(1)} %get-tuple-element.33.a_ref, bf16[256,256]{1,0:T(8,128)(2,1)S(1)} %copy-done, bf16[4,128,256]{2,1,0:T(8,128)(2,1)S(1)} %pad_maximum_fusion.wa_ref, f32[1,256]{1,0:T(1,128)S(1)} %bitcast.19, bf16[256,256]{1,0:T(8,128)(2,1)S(1)} %copy-done.1, ...), custom_call_target="tpu_custom_call" | custom-call | flops 671088640 | bytes 1048576 | tf_op jit(solution)/shard_map/rollout/pallas_call | solution.py:227
  44.6 1.8 %rollout.12 = (f32[512,256]{1,0:T(8,128)S(1)}, f32[512,256]{1,0:T(8,128)S(1)}) custom-call(bf16[512,1024]{1,0:T(8,128)(2,1)S(1)} %get-tuple-element.33.a_ref, bf16[256,256]{1,0:T(8,128)(2,1)S(1)} %copy-done, bf16[4,128,256]{2,1,0:T(8,128)(2,1)S(1)} %pad_maximum_fusion.wa_ref, f32[1,256]{1,0:T(1,128)S(1)} %bitcast.20, bf16[256,256]{1,0:T(8,128)(2,1)S(1)} %copy-done.1, ...), custom_call_target="tpu_custom_call" | custom-call | flops 671088640 | bytes 1048576 | tf_op jit(solution)/shard_map/rollout/pallas_call | solution.py:227
  46.4 0.1 collective-permute-start.11
  46.5 0.5 collective-permute-start.12
  47.0 1.8 %rollout.13 = (f32[512,256]{1,0:T(8,128)S(1)}, f32[512,256]{1,0:T(8,128)S(1)}) custom-call(bf16[512,1024]{1,0:T(8,128)(2,1)S(1)} %get-tuple-element.33.a_ref, bf16[256,256]{1,0:T(8,128)(2,1)S(1)} %copy-done, bf16[4,128,256]{2,1,0:T(8,128)(2,1)S(1)} %pad_maximum_fusion.wa_ref, f32[1,256]{1,0:T(1,128)S(1)} %bitcast.21, bf16[256,256]{1,0:T(8,128)(2,1)S(1)} %copy-done.1, ...), custom_call_target="tpu_custom_call" | custom-call | flops 671088640 | bytes 1048576 | tf_op jit(solution)/shard_map/rollout/pallas_call | solution.py:227
  48.8 2.0 %rollout.14 = (f32[512,256]{1,0:T(8,128)S(1)}, f32[512,256]{1,0:T(8,128)S(1)}) custom-call(bf16[512,1024]{1,0:T(8,128)(2,1)S(1)} %get-tuple-element.33.a_ref, bf16[256,256]{1,0:T(8,128)(2,1)S(1)} %copy-done, bf16[4,128,256]{2,1,0:T(8,128)(2,1)S(1)} %pad_maximum_fusion.wa_ref, f32[1,256]{1,0:T(1,128)S(1)} %bitcast.22, bf16[256,256]{1,0:T(8,128)(2,1)S(1)} %copy-done.1, ...), custom_call_target="tpu_custom_call" | custom-call | flops 671088640 | bytes 1048576 | tf_op jit(solution)/shard_map/rollout/pallas_call | solution.py:227
  50.8 2.8 %rollout.15 = f32[1,512]{1,0:T(1,128)} custom-call(bf16[512,1024]{1,0:T(8,128)(2,1)S(1)} %get-tuple-element.33.a_ref, bf16[256,256]{1,0:T(8,128)(2,1)S(1)} %copy-done, bf16[4,128,256]{2,1,0:T(8,128)(2,1)S(1)} %pad_maximum_fusion.wa_ref, f32[1,256]{1,0:T(1,128)S(1)} %bitcast.23, bf16[256,256]{1,0:T(8,128)(2,1)S(1)} %copy-done.1, f32[1,256]{1,0:T(1,128)S(1)} %bitcast.31, ...), custom_call_target="tpu_custom_call" | custom-call | flops 671088640 | bytes 1048576 | tf_op jit(solution)/shard_map/rollout/pallas_call | solution.py:227
  53.6 1.5 %finish.1 = (f32[1,1024]{1,0:T(1,128)}, f32[128,1024]{1,0:T(8,128)}) custom-call(s32[2]{0:T(128)S(1)} %pad_add_fusion.place_ref, f32[136,256]{1,0:T(8,128)S(1)} %combine.7.mine_ref, f32[136,256]{1,0:T(8,128)S(1)} %collective-permute-done.8.got_ref, f32[128,256]{1,0:T(8,128)S(1)} %slice_add_fusion.2.refs_0_, f32[128,256]{1,0:T(8,128)S(1)} %collective-permute-done.10.refs_1_, ...), custom_call_target="tpu_custom_call" | custom-call | tf_op jit(solution)/shard_map/finish/pallas_call | solution.py:264
  (29 shorter events, 0.5 us)
Async XLA Ops:
  3.3 3.4 %collective-permute-start.3 = (f32[520,256]{1,0:T(8,128)S(1)}, f32[520,256]{1,0:T(8,128)S(1)}, u32[]{:S(2)}, u32[]{:S(2)}) collective-permute-start(f32[520,256]{1,0:T(8,128)S(1)} %get-tuple-element.40.refs_2_), channel_id=1, source_target_pairs={{0,1},{1,0},{2,3},{3,2},{4,5},{5,4},{6,7},{7,6},{8,9},{9,8},{10,11... | collective-permute-start | bytes 1597448 | tf_op jit(solution)/shard_map/ppermute | solution.py:282
  5.1 6.2 %collective-permute-start = (f32[1024,256]{1,0:T(8,128)S(1)}, f32[1024,256]{1,0:T(8,128)S(1)}, u32[]{:S(2)}, u32[]{:S(2)}) collective-permute-start(f32[1024,256]{1,0:T(8,128)S(1)} %get-tuple-element.35), channel_id=1, source_target_pairs={{0,1},{1,0},{2,3},{3,2},{4,5},{5,4},{6,7},{7,6},{8,9},{9,8},{10,11... | collective-permute-start | bytes 3145736 | tf_op jit(solution)/shard_map/ppermute | solution.py:282
  5.2 4.2 %collective-permute-start.1 = (f32[512,256]{1,0:T(8,128)S(1)}, f32[512,256]{1,0:T(8,128)S(1)}, u32[]{:S(2)}, u32[]{:S(2)}) collective-permute-start(f32[512,256]{1,0:T(8,128)S(1)} %get-tuple-element.37), channel_id=1, source_target_pairs={{0,1},{1,0},{2,3},{3,2},{4,5},{5,4},{6,7},{7,6},{8,9},{9,8},{10,11... | collective-permute-start | bytes 1572872 | tf_op jit(solution)/shard_map/ppermute | solution.py:282
  6.8 9.9 %collective-permute-start.4 = (f32[520,256]{1,0:T(8,128)S(1)}, f32[520,256]{1,0:T(8,128)S(1)}, u32[]{:S(2)}, u32[]{:S(2)}) collective-permute-start(f32[520,256]{1,0:T(8,128)S(1)} %combine.4.refs_3_), channel_id=1, source_target_pairs={{0,4},{1,3},{2,6},{3,1},{4,0},{5,7},{6,2},{7,5},{8,12},{9,11},{10,... | collective-permute-start | bytes 1597448 | tf_op jit(solution)/shard_map/ppermute | solution.py:282
  9.5 15.8 %collective-permute-start.2 = (f32[512,256]{1,0:T(8,128)S(1)}, f32[512,256]{1,0:T(8,128)S(1)}, u32[]{:S(2)}, u32[]{:S(2)}) collective-permute-start(f32[512,256]{1,0:T(8,128)S(1)} %add.41), channel_id=1, source_target_pairs={{0,4},{1,3},{2,6},{3,1},{4,0},{5,7},{6,2},{7,5},{8,12},{9,11},{10,... | collective-permute-start | bytes 1572872 | tf_op jit(solution)/shard_map/ppermute | solution.py:282
  16.7 8.6 %collective-permute-start.6 = (f32[264,256]{1,0:T(8,128)S(1)}, f32[264,256]{1,0:T(8,128)S(1)}, u32[]{:S(2)}, u32[]{:S(2)}) collective-permute-start(f32[264,256]{1,0:T(8,128)S(1)} %combine.5.refs_4_), channel_id=1, source_target_pairs={{0,2},{1,5},{2,0},{3,7},{4,6},{5,1},{6,4},{7,3},{8,10},{9,13},{10,... | collective-permute-start | bytes 811016 | tf_op jit(solution)/shard_map/ppermute | solution.py:282
  18.8 0.7 %copy-start.5 = (bf16[32,256]{1,0:T(8,128)(2,1)S(1)}, bf16[32,256]{1,0:T(8,128)(2,1)}, u32[]{:S(2)}) copy-start(bf16[32,256]{1,0:T(8,128)(2,1)} %param.12) | copy-start | bytes 49156
  18.9 9.1 %collective-permute-start.5 = (f32[256,256]{1,0:T(8,128)S(1)}, f32[256,256]{1,0:T(8,128)S(1)}, u32[]{:S(2)}, u32[]{:S(2)}) collective-permute-start(f32[256,256]{1,0:T(8,128)S(1)} %slice_add_fusion), channel_id=1, source_target_pairs={{0,2},{1,5},{2,0},{3,7},{4,6},{5,1},{6,4},{7,3},{8,10},{9,13},{10,... | collective-permute-start | bytes 786440 | tf_op jit(solution)/shard_map/ppermute | solution.py:282
  25.3 6.6 %collective-permute-start.7 = (f32[136,256]{1,0:T(8,128)S(1)}, f32[136,256]{1,0:T(8,128)S(1)}, u32[]{:S(2)}, u32[]{:S(2)}) collective-permute-start(f32[136,256]{1,0:T(8,128)S(1)} %combine.6.refs_5_), channel_id=1, source_target_pairs={{0,8},{1,17},{2,10},{3,19},{4,12},{5,21},{6,14},{7,23},{8,0},{9,25... | collective-permute-start | bytes 417800 | tf_op jit(solution)/shard_map/ppermute | solution.py:282
  27.9 11.6 %collective-permute-start.9 = (f32[128,256]{1,0:T(8,128)S(1)}, f32[128,256]{1,0:T(8,128)S(1)}, u32[]{:S(2)}, u32[]{:S(2)}) collective-permute-start(f32[128,256]{1,0:T(8,128)S(1)} %slice_add_fusion.3), channel_id=1, source_target_pairs={{0,8},{1,17},{2,10},{3,19},{4,12},{5,21},{6,14},{7,23},{8,0},{9,25... | collective-permute-start | bytes 393224 | tf_op jit(solution)/shard_map/ppermute | solution.py:282
  31.9 7.5 %collective-permute-start.8 = (f32[136,256]{1,0:T(8,128)S(1)}, f32[136,256]{1,0:T(8,128)S(1)}, u32[]{:S(2)}, u32[]{:S(2)}) collective-permute-start(f32[136,256]{1,0:T(8,128)S(1)} %combine.7.mine_ref), channel_id=1, source_target_pairs={{0,16},{1,9},{2,18},{3,11},{4,20},{5,13},{6,22},{7,15},{8,24},{9,1... | collective-permute-start | bytes 417800 | tf_op jit(solution)/shard_map/ppermute | solution.py:282
  34.9 0.9 %copy-start = (bf16[256,256]{1,0:T(8,128)(2,1)S(1)}, bf16[256,256]{1,0:T(8,128)(2,1)}, u32[]{:S(2)}) copy-start(bf16[256,256]{1,0:T(8,128)(2,1)} %ws_ref.15) | copy-start | bytes 393220
  34.9 1.0 %copy-start.1 = (bf16[256,256]{1,0:T(8,128)(2,1)S(1)}, bf16[256,256]{1,0:T(8,128)(2,1)}, u32[]{:S(2)}) copy-start(bf16[256,256]{1,0:T(8,128)(2,1)} %wo_ref.15) | copy-start | bytes 393220
  34.9 1.0 %copy-start.3 = (f32[256]{0:T(256)S(1)}, f32[256]{0:T(256)}, u32[]{:S(2)}) copy-start(f32[256]{0:T(256)} %param.15) | copy-start | bytes 3076
  34.9 1.0 %copy-start.4 = (f32[256]{0:T(256)S(1)}, f32[256]{0:T(256)}, u32[]{:S(2)}) copy-start(f32[256]{0:T(256)} %param.10) | copy-start | bytes 3076
  35.0 0.9 %copy-start.2 = (f32[256]{0:T(256)S(1)}, f32[256]{0:T(256)}, u32[]{:S(2)}) copy-start(f32[256]{0:T(256)} %param.13) | copy-start | bytes 3076
  39.5 7.0 %collective-permute-start.10 = (f32[128,256]{1,0:T(8,128)S(1)}, f32[128,256]{1,0:T(8,128)S(1)}, u32[]{:S(2)}, u32[]{:S(2)}) collective-permute-start(f32[128,256]{1,0:T(8,128)S(1)} %slice_add_fusion.2.refs_0_), channel_id=1, source_target_pairs={{0,2},{1,3},{2,0},{3,1},{4,6},{5,7},{6,4},{7,5},{8,10},{9,11},{10,... | collective-permute-start | bytes 393224 | tf_op jit(solution)/shard_map/ppermute | solution.py:282
  46.4 7.2 %collective-permute-start.11 = (f32[128,256]{1,0:T(8,128)S(1)}, f32[128,256]{1,0:T(8,128)S(1)}, u32[]{:S(2)}, u32[]{:S(2)}) collective-permute-start(f32[128,256]{1,0:T(8,128)S(1)} %slice_add_fusion.2.refs_0_), channel_id=1, source_target_pairs={{0,1},{1,0},{2,3},{3,2},{4,5},{5,4},{6,7},{7,6},{8,9},{9,8},{10,11... | collective-permute-start | bytes 393224 | tf_op jit(solution)/shard_map/ppermute | solution.py:282
  46.5 7.1 %collective-permute-start.12 = (f32[128,256]{1,0:T(8,128)S(1)}, f32[128,256]{1,0:T(8,128)S(1)}, u32[]{:S(2)}, u32[]{:S(2)}) collective-permute-start(f32[128,256]{1,0:T(8,128)S(1)} %collective-permute-done.10.refs_1_), channel_id=1, source_target_pairs={{0,1},{1,0},{2,3},{3,2},{4,5},{5,4},{6,7},{7,6},{8,9},{9,8},{10,11... | collective-permute-start | bytes 393224 | tf_op jit(solution)/shard_map/ppermute | solution.py:282

commit v2 on v1

--- a/solution.py
+++ b/solution.py
@@ -10,7 +10,6 @@
 ALL = ("pop", "grp")
 CORE = (("grp", 1), ("grp", 1))
 VMEM = pl.BlockSpec(memory_space=pltpu.VMEM)
-SMEM = pl.BlockSpec(memory_space=pltpu.SMEM)
 HBM = pl.BlockSpec(memory_space=pltpu.HBM)
 PIECES = (4, 4, 4, 4, 4, 4, 4, 4)
 
@@ -64,10 +63,11 @@
         return out
 
 
-def moment_into(plan, place_ref, other, at_ref, a_ref, ranges, out_refs):
+def moment_into(plan, other, at_ref, a_ref, ranges, out_refs):
     rows, cols, side, run = plan.rows, plan.cols, plan.side, plan.run
-    here = place_ref[0] * side + place_ref[1] // 2
-    color = lax.rem(place_ref[1] + other, 2)
+    grp = lax.axis_index("grp")
+    here = lax.axis_index("pop") * side + grp // 2
+    color = lax.rem(grp + other, 2)
     where = {}
     for (lo, hi), ref in zip(ranges, out_refs, strict=True):
         for p in range(lo, hi):
@@ -86,7 +86,7 @@
             ref[pl.ds(at, rows), :] = got[k * rows : (k + 1) * rows]
 
 
-def first_kernel(plan, ranges, cuts, place_ref, w_hbm, a_hbm, a_ref, at_ref, *refs):
+def first_kernel(plan, ranges, cuts, w_hbm, a_hbm, a_ref, at_ref, *refs):
     out_refs, (w_ref, sems) = refs[:-2], refs[-2:]
     height = a_ref.shape[0] // cuts
     copies = [pltpu.make_async_copy(w_hbm, w_ref, sems.at[cuts])]
@@ -104,7 +104,7 @@
         for c in range(plan.width // 128):
             turned = jnp.transpose(a_ref[sl, c * 128 : (c + 1) * 128])
             at_ref[pl.ds(c * 128, 128), sl] = turned * wide[:, k * height : (k + 1) * height]
-    moment_into(plan, place_ref, 1, at_ref, a_ref, ranges, out_refs)
+    moment_into(plan, 1, at_ref, a_ref, ranges, out_refs)
     tall = jnp.broadcast_to(w, (16, w.shape[1])).astype(jnp.bfloat16)
     sums = jnp.dot(tall, a_ref[...], preferred_element_type=jnp.float32)
     lo, hi = ranges[0]
@@ -120,7 +120,7 @@
     return jax.ShapeDtypeStruct(shape, jnp.float32)
 
 
-def first(plan, place, weight, actions, ranges):
+def first(plan, weight, actions, ranges):
     count, width = actions.shape
     cuts = max(1, min(4, count // 128))
     held = jax.ShapeDtypeStruct((count, width), jnp.bfloat16)
@@ -130,31 +130,31 @@
     return pl.pallas_call(
         functools.partial(first_kernel, plan, ranges, cuts),
         out_shape=outs,
-        in_specs=[SMEM, HBM, HBM],
+        in_specs=[HBM, HBM],
         out_specs=[VMEM] * len(outs),
         scratch_shapes=[pltpu.VMEM((1, count), jnp.int32), pltpu.SemaphoreType.DMA((cuts + 1,))],
         compiler_params=pltpu.CompilerParams(vmem_limit_bytes=16 << 20),
         cost_estimate=pl.CostEstimate(flops=1 << 29, bytes_accessed=4 << 20, transcendentals=0),
         name="first",
-    )(place, pltpu.with_memory_space_constraint(weight, pltpu.HBM), pltpu.with_memory_space_constraint(actions, pltpu.HBM))
-
-
-def later_kernel(plan, theirs, ours, place_ref, at_ref, a_ref, *refs):
-    moment_into(plan, place_ref, 1, at_ref, a_ref, theirs, refs[: len(theirs)])
-    moment_into(plan, place_ref, 0, at_ref, a_ref, ours, refs[len(theirs) :])
-
-
-def later(plan, place, at, actions, theirs, ours):
+    )(pltpu.with_memory_space_constraint(weight, pltpu.HBM), pltpu.with_memory_space_constraint(actions, pltpu.HBM))
+
+
+def later_kernel(plan, theirs, ours, at_ref, a_ref, *refs):
+    moment_into(plan, 1, at_ref, a_ref, theirs, refs[: len(theirs)])
+    moment_into(plan, 0, at_ref, a_ref, ours, refs[len(theirs) :])
+
+
+def later(plan, at, actions, theirs, ours):
     outs = [f32((hi - lo) * plan.rows, plan.cols) for lo, hi in theirs + ours]
     got = pl.pallas_call(
         functools.partial(later_kernel, plan, theirs, ours),
         out_shape=outs,
-        in_specs=[SMEM, VMEM, VMEM],
+        in_specs=[VMEM, VMEM],
         out_specs=[VMEM] * len(outs),
         compiler_params=pltpu.CompilerParams(vmem_limit_bytes=16 << 20),
         cost_estimate=pl.CostEstimate(flops=1 << 29, bytes_accessed=4 << 20, transcendentals=0),
         name="later",
-    )(place, at, actions)
+    )(at, actions)
     return got[: len(theirs)], got[len(theirs) :]
 
 
@@ -236,7 +236,7 @@
     )(*operands)
 
 
-def finish_kernel(plan, ends, place_ref, mine_ref, got_ref, *refs):
+def finish_kernel(plan, ends, mine_ref, got_ref, *refs):
     pieces, (mean_ref, cov_ref, line_ref) = refs[:-3], refs[-3:]
     rows, cols, side = plan.rows, plan.cols, plan.side
     tail = mine_ref[pl.ds(ends[0], plan.tail), :] + got_ref[pl.ds(ends[1], plan.tail), :]
@@ -245,7 +245,7 @@
     inverse = 1.0 / count[:, 0:1]
     for k in range(lines):
         mean_ref[:, pl.ds(k * cols, cols)] = tail[k : k + 1] / count
-    pop, grp = place_ref[0], place_ref[1]
+    pop, grp = lax.axis_index("pop"), lax.axis_index("grp")
     start = pl.multiple_of(pop * rows // 128 * 128, 128)
     column = jnp.transpose(jnp.broadcast_to(mean_ref[:, pl.ds(start, 128)], (128, 128)))
     if rows < 128:
@@ -259,35 +259,34 @@
         cov_ref[:, sl] = piece[...] * inverse - left * mean_ref[:, sl]
 
 
-def finish(plan, place, mine, got, pieces):
+def finish(plan, mine, got, pieces):
     ends = (mine.shape[0] - plan.tail, got.shape[0] - plan.tail)
     return pl.pallas_call(
         functools.partial(finish_kernel, plan, ends),
         out_shape=(f32(1, plan.width), f32(plan.rows, plan.width)),
-        in_specs=[SMEM] + [VMEM] * (2 + len(pieces)),
+        in_specs=[VMEM] * (2 + len(pieces)),
         out_specs=(VMEM, VMEM),
         scratch_shapes=[pltpu.VMEM((128, 128), jnp.float32)],
         compiler_params=pltpu.CompilerParams(vmem_limit_bytes=8 << 20),
         name="finish",
-    )(place, mine, got, *pieces)
+    )(mine, got, *pieces)
 
 
 def on_device(plan, actions, elite_mask, init_state, w_state, w_action, bias, w_out, reward_vec):
     act = w_action.shape[0]
     steps = actions.shape[1] // act
     rows, phases, chunks = plan.rows, plan.phases, plan.chunks
-    place = jnp.stack([lax.axis_index("pop"), lax.axis_index("grp")]).astype(jnp.int32)
 
     def send(x, of):
         return lax.ppermute(x, ALL, plan.pairs(of))
 
     rest = [(0, plan.blocks // 2)]
-    actions, at, *outs = first(plan, place, elite_mask[None, :], actions, chunks[0])
+    actions, at, *outs = first(plan, elite_mask[None, :], actions, chunks[0])
     got = [(r, send(x, CORE)) for r, x in zip(chunks[0], outs, strict=True)]
     payload, received = outs[0], got[0][1]
-    own = dict(zip(chunks[0], later(plan, place, at, actions, [], chunks[0])[1], strict=True))
+    own = dict(zip(chunks[0], later(plan, at, actions, [], chunks[0])[1], strict=True))
     ours = [r for level in chunks[1:] for r in level]
-    theirs, more = later(plan, place, at, actions, rest, ours)
+    theirs, more = later(plan, at, actions, rest, ours)
     got.append((rest[0], send(theirs[0], CORE)))
     own.update(zip(ours, more, strict=True))
 
@@ -331,7 +330,7 @@
     for m in bits_of(plan.side):
         pieces += [send(x, (("grp", 2 * m), ("grp", 2 * m))) for x in pieces]
     pieces += [send(x, CORE) for x in pieces]
-    new_mean, covariance = finish(plan, place, payload, received, pieces)
+    new_mean, covariance = finish(plan, payload, received, pieces)
     return (new_mean[0], covariance, returns)
 
 

time: 55.3 us -> 53.2 us (0.962)
  Pallas kernels: 21.9 us -> 19.6 us
  starting transfers between devices: 15.5 us -> 16.2 us
    pallas_call x2, Pallas kernels: 2.28 us -> 1.17 us  [later(): pl.pallas_call(functools.partial(later_kernel, plan, theirs, ours), out_s...]
    ppermute x13, starting transfers between devices: 15.5 us -> 16.2 us  [send(): return lax.ppermute(x, ALL, plan.pairs(of))]
  transfers between devices with their start and end apart: 13 -> 13, of which waited for: 3 -> 3; matrix products, arithmetic and copies ran while one was open for 0% -> 0% of each run, Pallas kernels for 32% -> 31%
where the time goes in v2:
time: 53.2 us; the launch traced here: 53 us
  Pallas kernels  19.6 us (37%)
  starting transfers between devices  16.2 us (30%)
  waiting for transfers between devices  14.6 us (27%)
  local copies, waits for them, and re-layouts  1.5 us (3%)
  between operations  0.81 us (2%)
    ppermute x13, starting transfers between devices, send(): return lax.ppermute(x, ALL, plan.pairs(of))  16.2 us
    pallas_call x8, Pallas kernels, rollout(): pl.pallas_call(functools.partial(rollout_kernel, act, first, steps, scale...  15.3 us
    ppermute x13, waiting for transfers between devices, send(): return lax.ppermute(x, ALL, plan.pairs(of))  14.6 us
    pallas_call x1, Pallas kernels, first(): pl.pallas_call(functools.partial(first_kernel, plan, ranges, cuts), out_s...  2.04 us
    unnamed x12, local copies, waits for them, and re-layouts  1.48 us
    pallas_call x2, Pallas kernels, later(): pl.pallas_call(functools.partial(later_kernel, plan, theirs, ours), out_s...  1.17 us
  transfers between devices with their start and end apart: 13, of which 3 were waited for; matrix products, arithmetic and copies ran while one was open for 0% of the time, Pallas kernels for 31%

profile of v2, /device:TPU:0, one launch (start us, length us, event | category | flops | bytes accessed | tf_op | source)
XLA Modules:
  0.0 53.0 jit_solution(15566767219896767878)
XLA Ops:
  0.6 2.0 %first.1 = (bf16[512,1024]{1,0:T(8,128)(2,1)S(1)}, bf16[1024,512]{1,0:T(8,128)(2,1)S(1)}, f32[520,256]{1,0:T(8,128)S(1)}, f32[512,256]{1,0:T(8,128)S(1)}) custom-call(s32[1,512]{1,0:T(1,128)} %bitcast.33, bf16[512,1024]{1,0:T(8,128)(2,1)} %a_hbm.1), custom_call_target="tpu_custom_call" | custom-call | flops 536870912 | bytes 4194304 | tf_op jit(solution)/shard_map/first/pallas_call | solution.py:130
  2.7 0.6 %collective-permute-start.3 = (f32[520,256]{1,0:T(8,128)S(1)}, f32[520,256]{1,0:T(8,128)S(1)}, u32[]{:S(2)}, u32[]{:S(2)}) collective-permute-start(f32[520,256]{1,0:T(8,128)S(1)} %get-tuple-element.40.refs_2_), channel_id=1, source_target_pairs={{0,1},{1,0},{2,3},{3,2},{4,5},{5,4},{6,7},{7,6},{8,9},{9,8},{10,11... | collective-permute-start | bytes 1597448 | tf_op jit(solution)/shard_map/ppermute | solution.py:281
  3.2 0.7 %later.2 = (f32[1024,256]{1,0:T(8,128)S(1)}, f32[256,256]{1,0:T(8,128)S(1)}, f32[256,256]{1,0:T(8,128)S(1)}, f32[128,256]{1,0:T(8,128)S(1)}, f32[128,256]{1,0:T(...) custom-call(bf16[1024,512]{1,0:T(8,128)(2,1)S(1)} %get-tuple-element.32.at_ref, ...), custom_call_target="tpu_custom_call" | custom-call | flops 536870912 | bytes 4194304 | tf_op jit(solution)/shard_map/later/pallas_call | solution.py:149
  4.0 0.1 collective-permute-start
  4.1 0.5 collective-permute-start.1
  4.5 0.5 later.3
  5.1 2.7 %collective-permute-start.4 = (f32[520,256]{1,0:T(8,128)S(1)}, f32[520,256]{1,0:T(8,128)S(1)}, u32[]{:S(2)}, u32[]{:S(2)}) collective-permute-start(f32[520,256]{1,0:T(8,128)S(1)} %combine.4.refs_3_), channel_id=1, source_target_pairs={{0,4},{1,3},{2,6},{3,1},{4,0},{5,7},{6,2},{7,5},{8,12},{9,11},{10,... | collective-permute-start | bytes 1597448 | tf_op jit(solution)/shard_map/ppermute | solution.py:281
  7.8 0.1 add.41
  7.8 2.4 %collective-permute-start.2 = (f32[512,256]{1,0:T(8,128)S(1)}, f32[512,256]{1,0:T(8,128)S(1)}, u32[]{:S(2)}, u32[]{:S(2)}) collective-permute-start(f32[512,256]{1,0:T(8,128)S(1)} %add.41), channel_id=1, source_target_pairs={{0,4},{1,3},{2,6},{3,1},{4,0},{5,7},{6,2},{7,5},{8,12},{9,11},{10,... | collective-permute-start | bytes 1572872 | tf_op jit(solution)/shard_map/ppermute | solution.py:281
  10.2 4.8 %collective-permute-done.4.refs_2_.refs_4_ = f32[520,256]{1,0:T(8,128)S(1)} collective-permute-done((f32[520,256]{1,0:T(8,128)S(1)}, f32[520,256]{1,0:T(8,128)S(1)}, u32[]{:S(2)}, u32[]{:S(2)}) %collective-permute-start.4) | collective-permute-done | bytes 532512 | tf_op jit(solution)/shard_map/ppermute | solution.py:281
  15.1 2.1 %collective-permute-start.6 = (f32[264,256]{1,0:T(8,128)S(1)}, f32[264,256]{1,0:T(8,128)S(1)}, u32[]{:S(2)}, u32[]{:S(2)}) collective-permute-start(f32[264,256]{1,0:T(8,128)S(1)} %combine.5.refs_4_), channel_id=1, source_target_pairs={{0,2},{1,5},{2,0},{3,7},{4,6},{5,1},{6,4},{7,3},{8,10},{9,13},{10,... | collective-permute-start | bytes 811016 | tf_op jit(solution)/shard_map/ppermute | solution.py:281
  17.2 0.1 collective-permute-start.5
  17.3 0.6 %copy-done.5 = bf16[32,256]{1,0:T(8,128)(2,1)S(1)} copy-done((bf16[32,256]{1,0:T(8,128)(2,1)S(1)}, bf16[32,256]{1,0:T(8,128)(2,1)}, u32[]{:S(2)}) %copy-start.5) | copy-done | bytes 16408
  17.9 5.8 %collective-permute-done.2.refs_2_ = f32[512,256]{1,0:T(8,128)S(1)} collective-permute-done((f32[512,256]{1,0:T(8,128)S(1)}, f32[512,256]{1,0:T(8,128)S(1)}, u32[]{:S(2)}, u32[]{:S(2)}) %collective-permute-start.2) | collective-permute-done | bytes 524320 | tf_op jit(solution)/shard_map/ppermute | solution.py:281
  23.7 2.5 %collective-permute-start.7 = (f32[136,256]{1,0:T(8,128)S(1)}, f32[136,256]{1,0:T(8,128)S(1)}, u32[]{:S(2)}, u32[]{:S(2)}) collective-permute-start(f32[136,256]{1,0:T(8,128)S(1)} %combine.6.refs_5_), channel_id=1, source_target_pairs={{0,8},{1,17},{2,10},{3,19},{4,12},{5,21},{6,14},{7,23},{8,0},{9,25... | collective-permute-start | bytes 417800 | tf_op jit(solution)/shard_map/ppermute | solution.py:281
  26.3 0.1 collective-permute-start.9
  26.3 3.9 %collective-permute-done.7.refs_4_.refs_6_ = f32[136,256]{1,0:T(8,128)S(1)} collective-permute-done((f32[136,256]{1,0:T(8,128)S(1)}, f32[136,256]{1,0:T(8,128)S(1)}, u32[]{:S(2)}, u32[]{:S(2)}) %collective-permute-start.7) | collective-permute-done | bytes 139296 | tf_op jit(solution)/shard_map/ppermute | solution.py:281
  30.3 3.1 %collective-permute-start.8 = (f32[136,256]{1,0:T(8,128)S(1)}, f32[136,256]{1,0:T(8,128)S(1)}, u32[]{:S(2)}, u32[]{:S(2)}) collective-permute-start(f32[136,256]{1,0:T(8,128)S(1)} %combine.7.mine_ref), channel_id=1, source_target_pairs={{0,16},{1,9},{2,18},{3,11},{4,20},{5,13},{6,22},{7,15},{8,24},{9,1... | collective-permute-start | bytes 417800 | tf_op jit(solution)/shard_map/ppermute | solution.py:281
  33.5 0.8 %copy-done = bf16[256,256]{1,0:T(8,128)(2,1)S(1)} copy-done((bf16[256,256]{1,0:T(8,128)(2,1)S(1)}, bf16[256,256]{1,0:T(8,128)(2,1)}, u32[]{:S(2)}) %copy-start) | copy-done | bytes 131096
  34.4 1.7 %rollout.8 = (f32[512,256]{1,0:T(8,128)S(1)}, f32[512,256]{1,0:T(8,128)S(1)}) custom-call(bf16[512,1024]{1,0:T(8,128)(2,1)S(1)} %get-tuple-element.33.a_ref, bf16[256,256]{1,0:T(8,128)(2,1)S(1)} %copy-done, bf16[4,128,256]{2,1,0:T(8,128)(2,1)S(1)} %pad_maximum_fusion.wa_ref, f32[1,256]{1,0:T(1,128)S(1)} %bitcast.14, bf16[256,256]{1,0:T(8,128)(2,1)S(1)} %copy-done.1, ...), custom_call_target="tpu_custom_call" | custom-call | flops 671088640 | bytes 1048576 | tf_op jit(solution)/shard_map/rollout/pallas_call | solution.py:227
  36.2 1.7 %rollout.9 = (f32[512,256]{1,0:T(8,128)S(1)}, f32[512,256]{1,0:T(8,128)S(1)}) custom-call(bf16[512,1024]{1,0:T(8,128)(2,1)S(1)} %get-tuple-element.33.a_ref, bf16[256,256]{1,0:T(8,128)(2,1)S(1)} %copy-done, bf16[4,128,256]{2,1,0:T(8,128)(2,1)S(1)} %pad_maximum_fusion.wa_ref, f32[1,256]{1,0:T(1,128)S(1)} %bitcast.15, bf16[256,256]{1,0:T(8,128)(2,1)S(1)} %copy-done.1, ...), custom_call_target="tpu_custom_call" | custom-call | flops 671088640 | bytes 1048576 | tf_op jit(solution)/shard_map/rollout/pallas_call | solution.py:227
  37.9 0.1 slice_add_fusion.2.refs_0_
  38.0 1.6 %collective-permute-start.10 = (f32[128,256]{1,0:T(8,128)S(1)}, f32[128,256]{1,0:T(8,128)S(1)}, u32[]{:S(2)}, u32[]{:S(2)}) collective-permute-start(f32[128,256]{1,0:T(8,128)S(1)} %slice_add_fusion.2.refs_0_), channel_id=1, source_target_pairs={{0,2},{1,3},{2,0},{3,1},{4,6},{5,7},{6,4},{7,5},{8,10},{9,11},{10,... | collective-permute-start | bytes 393224 | tf_op jit(solution)/shard_map/ppermute | solution.py:281
  39.6 1.8 %rollout.10 = (f32[512,256]{1,0:T(8,128)S(1)}, f32[512,256]{1,0:T(8,128)S(1)}) custom-call(bf16[512,1024]{1,0:T(8,128)(2,1)S(1)} %get-tuple-element.33.a_ref, bf16[256,256]{1,0:T(8,128)(2,1)S(1)} %copy-done, bf16[4,128,256]{2,1,0:T(8,128)(2,1)S(1)} %pad_maximum_fusion.wa_ref, f32[1,256]{1,0:T(1,128)S(1)} %bitcast.16, bf16[256,256]{1,0:T(8,128)(2,1)S(1)} %copy-done.1, ...), custom_call_target="tpu_custom_call" | custom-call | flops 671088640 | bytes 1048576 | tf_op jit(solution)/shard_map/rollout/pallas_call | solution.py:227
  41.3 1.8 %rollout.11 = (f32[512,256]{1,0:T(8,128)S(1)}, f32[512,256]{1,0:T(8,128)S(1)}) custom-call(bf16[512,1024]{1,0:T(8,128)(2,1)S(1)} %get-tuple-element.33.a_ref, bf16[256,256]{1,0:T(8,128)(2,1)S(1)} %copy-done, bf16[4,128,256]{2,1,0:T(8,128)(2,1)S(1)} %pad_maximum_fusion.wa_ref, f32[1,256]{1,0:T(1,128)S(1)} %bitcast.17, bf16[256,256]{1,0:T(8,128)(2,1)S(1)} %copy-done.1, ...), custom_call_target="tpu_custom_call" | custom-call | flops 671088640 | bytes 1048576 | tf_op jit(solution)/shard_map/rollout/pallas_call | solution.py:227
  43.1 1.7 %rollout.12 = (f32[512,256]{1,0:T(8,128)S(1)}, f32[512,256]{1,0:T(8,128)S(1)}) custom-call(bf16[512,1024]{1,0:T(8,128)(2,1)S(1)} %get-tuple-element.33.a_ref, bf16[256,256]{1,0:T(8,128)(2,1)S(1)} %copy-done, bf16[4,128,256]{2,1,0:T(8,128)(2,1)S(1)} %pad_maximum_fusion.wa_ref, f32[1,256]{1,0:T(1,128)S(1)} %bitcast.18, bf16[256,256]{1,0:T(8,128)(2,1)S(1)} %copy-done.1, ...), custom_call_target="tpu_custom_call" | custom-call | flops 671088640 | bytes 1048576 | tf_op jit(solution)/shard_map/rollout/pallas_call | solution.py:227
  44.9 0.1 collective-permute-start.11
  45.0 0.5 collective-permute-start.12
  45.5 1.8 %rollout.13 = (f32[512,256]{1,0:T(8,128)S(1)}, f32[512,256]{1,0:T(8,128)S(1)}) custom-call(bf16[512,1024]{1,0:T(8,128)(2,1)S(1)} %get-tuple-element.33.a_ref, bf16[256,256]{1,0:T(8,128)(2,1)S(1)} %copy-done, bf16[4,128,256]{2,1,0:T(8,128)(2,1)S(1)} %pad_maximum_fusion.wa_ref, f32[1,256]{1,0:T(1,128)S(1)} %bitcast.19, bf16[256,256]{1,0:T(8,128)(2,1)S(1)} %copy-done.1, ...), custom_call_target="tpu_custom_call" | custom-call | flops 671088640 | bytes 1048576 | tf_op jit(solution)/shard_map/rollout/pallas_call | solution.py:227
  47.2 1.9 %rollout.14 = (f32[512,256]{1,0:T(8,128)S(1)}, f32[512,256]{1,0:T(8,128)S(1)}) custom-call(bf16[512,1024]{1,0:T(8,128)(2,1)S(1)} %get-tuple-element.33.a_ref, bf16[256,256]{1,0:T(8,128)(2,1)S(1)} %copy-done, bf16[4,128,256]{2,1,0:T(8,128)(2,1)S(1)} %pad_maximum_fusion.wa_ref, f32[1,256]{1,0:T(1,128)S(1)} %bitcast.20, bf16[256,256]{1,0:T(8,128)(2,1)S(1)} %copy-done.1, ...), custom_call_target="tpu_custom_call" | custom-call | flops 671088640 | bytes 1048576 | tf_op jit(solution)/shard_map/rollout/pallas_call | solution.py:227
  49.2 2.8 %rollout.15 = f32[1,512]{1,0:T(1,128)} custom-call(bf16[512,1024]{1,0:T(8,128)(2,1)S(1)} %get-tuple-element.33.a_ref, bf16[256,256]{1,0:T(8,128)(2,1)S(1)} %copy-done, bf16[4,128,256]{2,1,0:T(8,128)(2,1)S(1)} %pad_maximum_fusion.wa_ref, f32[1,256]{1,0:T(1,128)S(1)} %bitcast.21, bf16[256,256]{1,0:T(8,128)(2,1)S(1)} %copy-done.1, f32[1,256]{1,0:T(1,128)S(1)} %bitcast.29, ...), custom_call_target="tpu_custom_call" | custom-call | flops 671088640 | bytes 1048576 | tf_op jit(solution)/shard_map/rollout/pallas_call | solution.py:227
  52.0 1.0 %finish.1 = (f32[1,1024]{1,0:T(1,128)}, f32[128,1024]{1,0:T(8,128)}) custom-call(f32[136,256]{1,0:T(8,128)S(1)} %combine.7.mine_ref, f32[136,256]{1,0:T(8,128)S(1)} %collective-permute-done.8.got_ref, f32[128,256]{1,0:T(8,128)S(1)} %slice_add_fusion.2.refs_0_, f32[128,256]{1,0:T(8,128)S(1)} %collective-permute-done.10.refs_1_, ...), custom_call_target="tpu_custom_call" | custom-call | tf_op jit(solution)/shard_map/finish/pallas_call | solution.py:264
  (28 shorter events, 0.4 us)
Async XLA Ops:
  2.7 2.3 %collective-permute-start.3 = (f32[520,256]{1,0:T(8,128)S(1)}, f32[520,256]{1,0:T(8,128)S(1)}, u32[]{:S(2)}, u32[]{:S(2)}) collective-permute-start(f32[520,256]{1,0:T(8,128)S(1)} %get-tuple-element.40.refs_2_), channel_id=1, source_target_pairs={{0,1},{1,0},{2,3},{3,2},{4,5},{5,4},{6,7},{7,6},{8,9},{9,8},{10,11... | collective-permute-start | bytes 1597448 | tf_op jit(solution)/shard_map/ppermute | solution.py:281
  4.0 6.2 %collective-permute-start = (f32[1024,256]{1,0:T(8,128)S(1)}, f32[1024,256]{1,0:T(8,128)S(1)}, u32[]{:S(2)}, u32[]{:S(2)}) collective-permute-start(f32[1024,256]{1,0:T(8,128)S(1)} %get-tuple-element.35), channel_id=1, source_target_pairs={{0,1},{1,0},{2,3},{3,2},{4,5},{5,4},{6,7},{7,6},{8,9},{9,8},{10,11... | collective-permute-start | bytes 3145736 | tf_op jit(solution)/shard_map/ppermute | solution.py:281
  4.1 3.7 %collective-permute-start.1 = (f32[512,256]{1,0:T(8,128)S(1)}, f32[512,256]{1,0:T(8,128)S(1)}, u32[]{:S(2)}, u32[]{:S(2)}) collective-permute-start(f32[512,256]{1,0:T(8,128)S(1)} %get-tuple-element.37), channel_id=1, source_target_pairs={{0,1},{1,0},{2,3},{3,2},{4,5},{5,4},{6,7},{7,6},{8,9},{9,8},{10,11... | collective-permute-start | bytes 1572872 | tf_op jit(solution)/shard_map/ppermute | solution.py:281
  5.1 9.9 %collective-permute-start.4 = (f32[520,256]{1,0:T(8,128)S(1)}, f32[520,256]{1,0:T(8,128)S(1)}, u32[]{:S(2)}, u32[]{:S(2)}) collective-permute-start(f32[520,256]{1,0:T(8,128)S(1)} %combine.4.refs_3_), channel_id=1, source_target_pairs={{0,4},{1,3},{2,6},{3,1},{4,0},{5,7},{6,2},{7,5},{8,12},{9,11},{10,... | collective-permute-start | bytes 1597448 | tf_op jit(solution)/shard_map/ppermute | solution.py:281
  7.8 15.9 %collective-permute-start.2 = (f32[512,256]{1,0:T(8,128)S(1)}, f32[512,256]{1,0:T(8,128)S(1)}, u32[]{:S(2)}, u32[]{:S(2)}) collective-permute-start(f32[512,256]{1,0:T(8,128)S(1)} %add.41), channel_id=1, source_target_pairs={{0,4},{1,3},{2,6},{3,1},{4,0},{5,7},{6,2},{7,5},{8,12},{9,11},{10,... | collective-permute-start | bytes 1572872 | tf_op jit(solution)/shard_map/ppermute | solution.py:281
  15.1 8.7 %collective-permute-start.6 = (f32[264,256]{1,0:T(8,128)S(1)}, f32[264,256]{1,0:T(8,128)S(1)}, u32[]{:S(2)}, u32[]{:S(2)}) collective-permute-start(f32[264,256]{1,0:T(8,128)S(1)} %combine.5.refs_4_), channel_id=1, source_target_pairs={{0,2},{1,5},{2,0},{3,7},{4,6},{5,1},{6,4},{7,3},{8,10},{9,13},{10,... | collective-permute-start | bytes 811016 | tf_op jit(solution)/shard_map/ppermute | solution.py:281
  17.2 0.7 %copy-start.5 = (bf16[32,256]{1,0:T(8,128)(2,1)S(1)}, bf16[32,256]{1,0:T(8,128)(2,1)}, u32[]{:S(2)}) copy-start(bf16[32,256]{1,0:T(8,128)(2,1)} %param.12) | copy-start | bytes 49156
  17.2 9.1 %collective-permute-start.5 = (f32[256,256]{1,0:T(8,128)S(1)}, f32[256,256]{1,0:T(8,128)S(1)}, u32[]{:S(2)}, u32[]{:S(2)}) collective-permute-start(f32[256,256]{1,0:T(8,128)S(1)} %slice_add_fusion), channel_id=1, source_target_pairs={{0,2},{1,5},{2,0},{3,7},{4,6},{5,1},{6,4},{7,3},{8,10},{9,13},{10,... | collective-permute-start | bytes 786440 | tf_op jit(solution)/shard_map/ppermute | solution.py:281
  23.7 6.5 %collective-permute-start.7 = (f32[136,256]{1,0:T(8,128)S(1)}, f32[136,256]{1,0:T(8,128)S(1)}, u32[]{:S(2)}, u32[]{:S(2)}) collective-permute-start(f32[136,256]{1,0:T(8,128)S(1)} %combine.6.refs_5_), channel_id=1, source_target_pairs={{0,8},{1,17},{2,10},{3,19},{4,12},{5,21},{6,14},{7,23},{8,0},{9,25... | collective-permute-start | bytes 417800 | tf_op jit(solution)/shard_map/ppermute | solution.py:281
  26.3 11.7 %collective-permute-start.9 = (f32[128,256]{1,0:T(8,128)S(1)}, f32[128,256]{1,0:T(8,128)S(1)}, u32[]{:S(2)}, u32[]{:S(2)}) collective-permute-start(f32[128,256]{1,0:T(8,128)S(1)} %slice_add_fusion.3), channel_id=1, source_target_pairs={{0,8},{1,17},{2,10},{3,19},{4,12},{5,21},{6,14},{7,23},{8,0},{9,25... | collective-permute-start | bytes 393224 | tf_op jit(solution)/shard_map/ppermute | solution.py:281
  30.3 7.6 %collective-permute-start.8 = (f32[136,256]{1,0:T(8,128)S(1)}, f32[136,256]{1,0:T(8,128)S(1)}, u32[]{:S(2)}, u32[]{:S(2)}) collective-permute-start(f32[136,256]{1,0:T(8,128)S(1)} %combine.7.mine_ref), channel_id=1, source_target_pairs={{0,16},{1,9},{2,18},{3,11},{4,20},{5,13},{6,22},{7,15},{8,24},{9,1... | collective-permute-start | bytes 417800 | tf_op jit(solution)/shard_map/ppermute | solution.py:281
  33.4 0.9 %copy-start = (bf16[256,256]{1,0:T(8,128)(2,1)S(1)}, bf16[256,256]{1,0:T(8,128)(2,1)}, u32[]{:S(2)}) copy-start(bf16[256,256]{1,0:T(8,128)(2,1)} %ws_ref.15) | copy-start | bytes 393220
  33.4 1.0 %copy-start.1 = (bf16[256,256]{1,0:T(8,128)(2,1)S(1)}, bf16[256,256]{1,0:T(8,128)(2,1)}, u32[]{:S(2)}) copy-start(bf16[256,256]{1,0:T(8,128)(2,1)} %wo_ref.15) | copy-start | bytes 393220
  33.4 1.0 %copy-start.3 = (f32[256]{0:T(256)S(1)}, f32[256]{0:T(256)}, u32[]{:S(2)}) copy-start(f32[256]{0:T(256)} %param.15) | copy-start | bytes 3076
  33.5 1.0 %copy-start.4 = (f32[256]{0:T(256)S(1)}, f32[256]{0:T(256)}, u32[]{:S(2)}) copy-start(f32[256]{0:T(256)} %param.10) | copy-start | bytes 3076
  33.5 0.9 %copy-start.2 = (f32[256]{0:T(256)S(1)}, f32[256]{0:T(256)}, u32[]{:S(2)}) copy-start(f32[256]{0:T(256)} %param.13) | copy-start | bytes 3076
  38.0 6.9 %collective-permute-start.10 = (f32[128,256]{1,0:T(8,128)S(1)}, f32[128,256]{1,0:T(8,128)S(1)}, u32[]{:S(2)}, u32[]{:S(2)}) collective-permute-start(f32[128,256]{1,0:T(8,128)S(1)} %slice_add_fusion.2.refs_0_), channel_id=1, source_target_pairs={{0,2},{1,3},{2,0},{3,1},{4,6},{5,7},{6,4},{7,5},{8,10},{9,11},{10,... | collective-permute-start | bytes 393224 | tf_op jit(solution)/shard_map/ppermute | solution.py:281
  44.9 7.1 %collective-permute-start.11 = (f32[128,256]{1,0:T(8,128)S(1)}, f32[128,256]{1,0:T(8,128)S(1)}, u32[]{:S(2)}, u32[]{:S(2)}) collective-permute-start(f32[128,256]{1,0:T(8,128)S(1)} %slice_add_fusion.2.refs_0_), channel_id=1, source_target_pairs={{0,1},{1,0},{2,3},{3,2},{4,5},{5,4},{6,7},{7,6},{8,9},{9,8},{10,11... | collective-permute-start | bytes 393224 | tf_op jit(solution)/shard_map/ppermute | solution.py:281
  45.0 7.0 %collective-permute-start.12 = (f32[128,256]{1,0:T(8,128)S(1)}, f32[128,256]{1,0:T(8,128)S(1)}, u32[]{:S(2)}, u32[]{:S(2)}) collective-permute-start(f32[128,256]{1,0:T(8,128)S(1)} %collective-permute-done.10.refs_1_), channel_id=1, source_target_pairs={{0,1},{1,0},{2,3},{3,2},{4,5},{5,4},{6,7},{7,6},{8,9},{9,8},{10,11... | collective-permute-start | bytes 393224 | tf_op jit(solution)/shard_map/ppermute | solution.py:281

commit v3 on v2

--- a/solution.py
+++ b/solution.py
@@ -43,8 +43,9 @@
         size = self.blocks
         while size > 1:
             size //= 2
-            self.chunks.append([(size + size // 2, 2 * size), (size, size + size // 2)] if size > 1 else [(1, 2)])
-        self.chunks.append([(0, 1)])
+            half = [list(range(size + size // 2, 2 * size)), list(range(size, size + size // 2))]
+            self.chunks.append(half if size > 1 else [[1]])
+        self.chunks.append([[0]])
 
     def mask(self, order, p):
         pop = grp = 0
@@ -69,9 +70,9 @@
     here = lax.axis_index("pop") * side + grp // 2
     color = lax.rem(grp + other, 2)
     where = {}
-    for (lo, hi), ref in zip(ranges, out_refs, strict=True):
-        for p in range(lo, hi):
-            where[p] = (ref, (p - lo) * rows)
+    for positions, ref in zip(ranges, out_refs, strict=True):
+        for i, p in enumerate(positions):
+            where[p] = (ref, i * rows)
     for first in range(0, plan.blocks, run):
         if first not in where:
             continue
@@ -107,8 +108,7 @@
     moment_into(plan, 1, at_ref, a_ref, ranges, out_refs)
     tall = jnp.broadcast_to(w, (16, w.shape[1])).astype(jnp.bfloat16)
     sums = jnp.dot(tall, a_ref[...], preferred_element_type=jnp.float32)
-    lo, hi = ranges[0]
-    base, cols = (hi - lo) * plan.rows, plan.cols
+    base, cols = len(ranges[0]) * plan.rows, plan.cols
     for k in range(plan.width // cols):
         out_refs[0][pl.ds(base + k, 1), :] = sums[0:1, k * cols : (k + 1) * cols]
     left = plan.tail - plan.width // cols
@@ -126,7 +126,7 @@
     held = jax.ShapeDtypeStruct((count, width), jnp.bfloat16)
     turned = jax.ShapeDtypeStruct((width, count), jnp.bfloat16)
     outs = [held, turned]
-    outs += [f32((hi - lo) * plan.rows + (0 if i else plan.tail), plan.cols) for i, (lo, hi) in enumerate(ranges)]
+    outs += [f32(len(r) * plan.rows + (0 if i else plan.tail), plan.cols) for i, r in enumerate(ranges)]
     return pl.pallas_call(
         functools.partial(first_kernel, plan, ranges, cuts),
         out_shape=outs,
@@ -145,7 +145,7 @@
 
 
 def later(plan, at, actions, theirs, ours):
-    outs = [f32((hi - lo) * plan.rows, plan.cols) for lo, hi in theirs + ours]
+    outs = [f32(len(r) * plan.rows, plan.cols) for r in theirs + ours]
     got = pl.pallas_call(
         functools.partial(later_kernel, plan, theirs, ours),
         out_shape=outs,
@@ -280,22 +280,28 @@
     def send(x, of):
         return lax.ppermute(x, ALL, plan.pairs(of))
 
-    rest = [(0, plan.blocks // 2)]
+    rest = list(range(plan.blocks // 2))
     actions, at, *outs = first(plan, elite_mask[None, :], actions, chunks[0])
     got = [(r, send(x, CORE)) for r, x in zip(chunks[0], outs, strict=True)]
     payload, received = outs[0], got[0][1]
-    own = dict(zip(chunks[0], later(plan, at, actions, [], chunks[0])[1], strict=True))
+    mine = later(plan, at, actions, [], chunks[0])[1]
     ours = [r for level in chunks[1:] for r in level]
-    theirs, more = later(plan, at, actions, rest, ours)
-    got.append((rest[0], send(theirs[0], CORE)))
-    own.update(zip(ours, more, strict=True))
-
-    def terms(lo, hi):
-        return [(x, (lo - a) * rows) for (a, b), x in got if a <= lo and hi <= b]
-
-    def total(lo, hi):
-        out = own[lo, hi]
-        for x, at in terms(lo, hi):
+    theirs, more = later(plan, at, actions, [rest], ours)
+    got.append((rest, send(theirs[0], CORE)))
+    own = {tuple(r): x for r, x in zip(chunks[0] + ours, list(mine) + list(more), strict=True)}
+
+    def terms(positions):
+        out = []
+        for held, x in got:
+            if set(positions) <= set(held):
+                at = held.index(positions[0])
+                assert held[at : at + len(positions)] == positions
+                out.append((x, at * rows))
+        return out
+
+    def total(positions):
+        out = own[tuple(positions)]
+        for x, at in terms(positions):
             out = out + x[at : at + out.shape[0]]
         return out
 
@@ -314,19 +320,15 @@
         of = (plan.orders[0][k], plan.orders[1][k])
         base = 1 << (phases - 1 - k)
         sent = []
-        for i, (lo, hi) in enumerate(chunks[k]):
+        for i, positions in enumerate(chunks[k]):
             if i == 0:
-                payload = combine(plan, own[lo, hi], terms(lo, hi), payload, received)
-                x = payload
+                payload = combine(plan, own[tuple(positions)], terms(positions), payload, received)
+                received = x = send(payload, of)
             else:
-                x = total(lo, hi)
-            x = send(x, of)
-            if i == 0:
-                received = x
-            at = 0 if hi - lo == base else lo - base
-            sent.append(((at, at + hi - lo), x))
+                x = send(total(positions), of)
+            sent.append(([p - base for p in positions], x))
         got += sent
-    pieces = [total(0, 1)]
+    pieces = [total([0])]
     for m in bits_of(plan.side):
         pieces += [send(x, (("grp", 2 * m), ("grp", 2 * m))) for x in pieces]
     pieces += [send(x, CORE) for x in pieces]

time: 53.2 us -> 53.2 us (level)
  no operation moved by 1% of the time
where the time goes in v3:
time: 53.2 us; the launch traced here: 53 us
  Pallas kernels  19.6 us (37%)
  starting transfers between devices  16.2 us (30%)
  waiting for transfers between devices  14.6 us (27%)
  local copies, waits for them, and re-layouts  1.5 us (3%)
  between operations  0.81 us (2%)
    ppermute x13, starting transfers between devices, send(): return lax.ppermute(x, ALL, plan.pairs(of))  16.2 us
    pallas_call x8, Pallas kernels, rollout(): pl.pallas_call(functools.partial(rollout_kernel, act, first, steps, scale...  15.3 us
    ppermute x13, waiting for transfers between devices, send(): return lax.ppermute(x, ALL, plan.pairs(of))  14.6 us
    pallas_call x1, Pallas kernels, first(): pl.pallas_call(functools.partial(first_kernel, plan, ranges, cuts), out_s...  2.04 us
    unnamed x12, local copies, waits for them, and re-layouts  1.48 us
    pallas_call x2, Pallas kernels, later(): pl.pallas_call(functools.partial(later_kernel, plan, theirs, ours), out_s...  1.17 us
  transfers between devices with their start and end apart: 13, of which 3 were waited for; matrix products, arithmetic and copies ran while one was open for 0% of the time, Pallas kernels for 31%

profile of v3, /device:TPU:0, one launch (start us, length us, event | category | flops | bytes accessed | tf_op | source)
XLA Modules:
  0.0 53.0 jit_solution(15566767219896767878)
XLA Ops:
  0.6 2.0 %first.1 = (bf16[512,1024]{1,0:T(8,128)(2,1)S(1)}, bf16[1024,512]{1,0:T(8,128)(2,1)S(1)}, f32[520,256]{1,0:T(8,128)S(1)}, f32[512,256]{1,0:T(8,128)S(1)}) custom-call(s32[1,512]{1,0:T(1,128)} %bitcast.33, bf16[512,1024]{1,0:T(8,128)(2,1)} %a_hbm.1), custom_call_target="tpu_custom_call" | custom-call | flops 536870912 | bytes 4194304 | tf_op jit(solution)/shard_map/first/pallas_call | solution.py:130
  2.7 0.6 %collective-permute-start.3 = (f32[520,256]{1,0:T(8,128)S(1)}, f32[520,256]{1,0:T(8,128)S(1)}, u32[]{:S(2)}, u32[]{:S(2)}) collective-permute-start(f32[520,256]{1,0:T(8,128)S(1)} %get-tuple-element.40.refs_2_), channel_id=1, source_target_pairs={{0,1},{1,0},{2,3},{3,2},{4,5},{5,4},{6,7},{7,6},{8,9},{9,8},{10,11... | collective-permute-start | bytes 1597448 | tf_op jit(solution)/shard_map/ppermute | solution.py:281
  3.2 0.7 %later.2 = (f32[1024,256]{1,0:T(8,128)S(1)}, f32[256,256]{1,0:T(8,128)S(1)}, f32[256,256]{1,0:T(8,128)S(1)}, f32[128,256]{1,0:T(8,128)S(1)}, f32[128,256]{1,0:T(...) custom-call(bf16[1024,512]{1,0:T(8,128)(2,1)S(1)} %get-tuple-element.32.at_ref, ...), custom_call_target="tpu_custom_call" | custom-call | flops 536870912 | bytes 4194304 | tf_op jit(solution)/shard_map/later/pallas_call | solution.py:149
  4.0 0.1 collective-permute-start
  4.1 0.5 collective-permute-start.1
  4.5 0.5 later.3
  5.1 2.7 %collective-permute-start.4 = (f32[520,256]{1,0:T(8,128)S(1)}, f32[520,256]{1,0:T(8,128)S(1)}, u32[]{:S(2)}, u32[]{:S(2)}) collective-permute-start(f32[520,256]{1,0:T(8,128)S(1)} %combine.4.refs_3_), channel_id=1, source_target_pairs={{0,4},{1,3},{2,6},{3,1},{4,0},{5,7},{6,2},{7,5},{8,12},{9,11},{10,... | collective-permute-start | bytes 1597448 | tf_op jit(solution)/shard_map/ppermute | solution.py:281
  7.8 0.1 add.41
  7.8 2.4 %collective-permute-start.2 = (f32[512,256]{1,0:T(8,128)S(1)}, f32[512,256]{1,0:T(8,128)S(1)}, u32[]{:S(2)}, u32[]{:S(2)}) collective-permute-start(f32[512,256]{1,0:T(8,128)S(1)} %add.41), channel_id=1, source_target_pairs={{0,4},{1,3},{2,6},{3,1},{4,0},{5,7},{6,2},{7,5},{8,12},{9,11},{10,... | collective-permute-start | bytes 1572872 | tf_op jit(solution)/shard_map/ppermute | solution.py:281
  10.2 4.8 %collective-permute-done.4.refs_2_.refs_4_ = f32[520,256]{1,0:T(8,128)S(1)} collective-permute-done((f32[520,256]{1,0:T(8,128)S(1)}, f32[520,256]{1,0:T(8,128)S(1)}, u32[]{:S(2)}, u32[]{:S(2)}) %collective-permute-start.4) | collective-permute-done | bytes 532512 | tf_op jit(solution)/shard_map/ppermute | solution.py:281
  15.1 2.1 %collective-permute-start.6 = (f32[264,256]{1,0:T(8,128)S(1)}, f32[264,256]{1,0:T(8,128)S(1)}, u32[]{:S(2)}, u32[]{:S(2)}) collective-permute-start(f32[264,256]{1,0:T(8,128)S(1)} %combine.5.refs_4_), channel_id=1, source_target_pairs={{0,2},{1,5},{2,0},{3,7},{4,6},{5,1},{6,4},{7,3},{8,10},{9,13},{10,... | collective-permute-start | bytes 811016 | tf_op jit(solution)/shard_map/ppermute | solution.py:281
  17.2 0.1 collective-permute-start.5
  17.3 0.6 %copy-done.5 = bf16[32,256]{1,0:T(8,128)(2,1)S(1)} copy-done((bf16[32,256]{1,0:T(8,128)(2,1)S(1)}, bf16[32,256]{1,0:T(8,128)(2,1)}, u32[]{:S(2)}) %copy-start.5) | copy-done | bytes 16408
  17.9 5.8 %collective-permute-done.2.refs_2_ = f32[512,256]{1,0:T(8,128)S(1)} collective-permute-done((f32[512,256]{1,0:T(8,128)S(1)}, f32[512,256]{1,0:T(8,128)S(1)}, u32[]{:S(2)}, u32[]{:S(2)}) %collective-permute-start.2) | collective-permute-done | bytes 524320 | tf_op jit(solution)/shard_map/ppermute | solution.py:281
  23.7 2.5 %collective-permute-start.7 = (f32[136,256]{1,0:T(8,128)S(1)}, f32[136,256]{1,0:T(8,128)S(1)}, u32[]{:S(2)}, u32[]{:S(2)}) collective-permute-start(f32[136,256]{1,0:T(8,128)S(1)} %combine.6.refs_5_), channel_id=1, source_target_pairs={{0,8},{1,17},{2,10},{3,19},{4,12},{5,21},{6,14},{7,23},{8,0},{9,25... | collective-permute-start | bytes 417800 | tf_op jit(solution)/shard_map/ppermute | solution.py:281
  26.3 0.1 collective-permute-start.9
  26.3 3.9 %collective-permute-done.7.refs_4_.refs_6_ = f32[136,256]{1,0:T(8,128)S(1)} collective-permute-done((f32[136,256]{1,0:T(8,128)S(1)}, f32[136,256]{1,0:T(8,128)S(1)}, u32[]{:S(2)}, u32[]{:S(2)}) %collective-permute-start.7) | collective-permute-done | bytes 139296 | tf_op jit(solution)/shard_map/ppermute | solution.py:281
  30.3 3.1 %collective-permute-start.8 = (f32[136,256]{1,0:T(8,128)S(1)}, f32[136,256]{1,0:T(8,128)S(1)}, u32[]{:S(2)}, u32[]{:S(2)}) collective-permute-start(f32[136,256]{1,0:T(8,128)S(1)} %combine.7.mine_ref), channel_id=1, source_target_pairs={{0,16},{1,9},{2,18},{3,11},{4,20},{5,13},{6,22},{7,15},{8,24},{9,1... | collective-permute-start | bytes 417800 | tf_op jit(solution)/shard_map/ppermute | solution.py:281
  33.5 0.8 %copy-done = bf16[256,256]{1,0:T(8,128)(2,1)S(1)} copy-done((bf16[256,256]{1,0:T(8,128)(2,1)S(1)}, bf16[256,256]{1,0:T(8,128)(2,1)}, u32[]{:S(2)}) %copy-start) | copy-done | bytes 131096
  34.4 1.7 %rollout.8 = (f32[512,256]{1,0:T(8,128)S(1)}, f32[512,256]{1,0:T(8,128)S(1)}) custom-call(bf16[512,1024]{1,0:T(8,128)(2,1)S(1)} %get-tuple-element.33.a_ref, bf16[256,256]{1,0:T(8,128)(2,1)S(1)} %copy-done, bf16[4,128,256]{2,1,0:T(8,128)(2,1)S(1)} %pad_maximum_fusion.wa_ref, f32[1,256]{1,0:T(1,128)S(1)} %bitcast.14, bf16[256,256]{1,0:T(8,128)(2,1)S(1)} %copy-done.1, ...), custom_call_target="tpu_custom_call" | custom-call | flops 671088640 | bytes 1048576 | tf_op jit(solution)/shard_map/rollout/pallas_call | solution.py:227
  36.2 1.7 %rollout.9 = (f32[512,256]{1,0:T(8,128)S(1)}, f32[512,256]{1,0:T(8,128)S(1)}) custom-call(bf16[512,1024]{1,0:T(8,128)(2,1)S(1)} %get-tuple-element.33.a_ref, bf16[256,256]{1,0:T(8,128)(2,1)S(1)} %copy-done, bf16[4,128,256]{2,1,0:T(8,128)(2,1)S(1)} %pad_maximum_fusion.wa_ref, f32[1,256]{1,0:T(1,128)S(1)} %bitcast.15, bf16[256,256]{1,0:T(8,128)(2,1)S(1)} %copy-done.1, ...), custom_call_target="tpu_custom_call" | custom-call | flops 671088640 | bytes 1048576 | tf_op jit(solution)/shard_map/rollout/pallas_call | solution.py:227
  37.9 0.1 slice_add_fusion.2.refs_0_
  38.0 1.6 %collective-permute-start.10 = (f32[128,256]{1,0:T(8,128)S(1)}, f32[128,256]{1,0:T(8,128)S(1)}, u32[]{:S(2)}, u32[]{:S(2)}) collective-permute-start(f32[128,256]{1,0:T(8,128)S(1)} %slice_add_fusion.2.refs_0_), channel_id=1, source_target_pairs={{0,2},{1,3},{2,0},{3,1},{4,6},{5,7},{6,4},{7,5},{8,10},{9,11},{10,... | collective-permute-start | bytes 393224 | tf_op jit(solution)/shard_map/ppermute | solution.py:281
  39.6 1.8 %rollout.10 = (f32[512,256]{1,0:T(8,128)S(1)}, f32[512,256]{1,0:T(8,128)S(1)}) custom-call(bf16[512,1024]{1,0:T(8,128)(2,1)S(1)} %get-tuple-element.33.a_ref, bf16[256,256]{1,0:T(8,128)(2,1)S(1)} %copy-done, bf16[4,128,256]{2,1,0:T(8,128)(2,1)S(1)} %pad_maximum_fusion.wa_ref, f32[1,256]{1,0:T(1,128)S(1)} %bitcast.16, bf16[256,256]{1,0:T(8,128)(2,1)S(1)} %copy-done.1, ...), custom_call_target="tpu_custom_call" | custom-call | flops 671088640 | bytes 1048576 | tf_op jit(solution)/shard_map/rollout/pallas_call | solution.py:227
  41.3 1.8 %rollout.11 = (f32[512,256]{1,0:T(8,128)S(1)}, f32[512,256]{1,0:T(8,128)S(1)}) custom-call(bf16[512,1024]{1,0:T(8,128)(2,1)S(1)} %get-tuple-element.33.a_ref, bf16[256,256]{1,0:T(8,128)(2,1)S(1)} %copy-done, bf16[4,128,256]{2,1,0:T(8,128)(2,1)S(1)} %pad_maximum_fusion.wa_ref, f32[1,256]{1,0:T(1,128)S(1)} %bitcast.17, bf16[256,256]{1,0:T(8,128)(2,1)S(1)} %copy-done.1, ...), custom_call_target="tpu_custom_call" | custom-call | flops 671088640 | bytes 1048576 | tf_op jit(solution)/shard_map/rollout/pallas_call | solution.py:227
  43.1 1.7 %rollout.12 = (f32[512,256]{1,0:T(8,128)S(1)}, f32[512,256]{1,0:T(8,128)S(1)}) custom-call(bf16[512,1024]{1,0:T(8,128)(2,1)S(1)} %get-tuple-element.33.a_ref, bf16[256,256]{1,0:T(8,128)(2,1)S(1)} %copy-done, bf16[4,128,256]{2,1,0:T(8,128)(2,1)S(1)} %pad_maximum_fusion.wa_ref, f32[1,256]{1,0:T(1,128)S(1)} %bitcast.18, bf16[256,256]{1,0:T(8,128)(2,1)S(1)} %copy-done.1, ...), custom_call_target="tpu_custom_call" | custom-call | flops 671088640 | bytes 1048576 | tf_op jit(solution)/shard_map/rollout/pallas_call | solution.py:227
  44.9 0.1 collective-permute-start.11
  45.0 0.5 collective-permute-start.12
  45.5 1.8 %rollout.13 = (f32[512,256]{1,0:T(8,128)S(1)}, f32[512,256]{1,0:T(8,128)S(1)}) custom-call(bf16[512,1024]{1,0:T(8,128)(2,1)S(1)} %get-tuple-element.33.a_ref, bf16[256,256]{1,0:T(8,128)(2,1)S(1)} %copy-done, bf16[4,128,256]{2,1,0:T(8,128)(2,1)S(1)} %pad_maximum_fusion.wa_ref, f32[1,256]{1,0:T(1,128)S(1)} %bitcast.19, bf16[256,256]{1,0:T(8,128)(2,1)S(1)} %copy-done.1, ...), custom_call_target="tpu_custom_call" | custom-call | flops 671088640 | bytes 1048576 | tf_op jit(solution)/shard_map/rollout/pallas_call | solution.py:227
  47.2 1.9 %rollout.14 = (f32[512,256]{1,0:T(8,128)S(1)}, f32[512,256]{1,0:T(8,128)S(1)}) custom-call(bf16[512,1024]{1,0:T(8,128)(2,1)S(1)} %get-tuple-element.33.a_ref, bf16[256,256]{1,0:T(8,128)(2,1)S(1)} %copy-done, bf16[4,128,256]{2,1,0:T(8,128)(2,1)S(1)} %pad_maximum_fusion.wa_ref, f32[1,256]{1,0:T(1,128)S(1)} %bitcast.20, bf16[256,256]{1,0:T(8,128)(2,1)S(1)} %copy-done.1, ...), custom_call_target="tpu_custom_call" | custom-call | flops 671088640 | bytes 1048576 | tf_op jit(solution)/shard_map/rollout/pallas_call | solution.py:227
  49.2 2.8 %rollout.15 = f32[1,512]{1,0:T(1,128)} custom-call(bf16[512,1024]{1,0:T(8,128)(2,1)S(1)} %get-tuple-element.33.a_ref, bf16[256,256]{1,0:T(8,128)(2,1)S(1)} %copy-done, bf16[4,128,256]{2,1,0:T(8,128)(2,1)S(1)} %pad_maximum_fusion.wa_ref, f32[1,256]{1,0:T(1,128)S(1)} %bitcast.21, bf16[256,256]{1,0:T(8,128)(2,1)S(1)} %copy-done.1, f32[1,256]{1,0:T(1,128)S(1)} %bitcast.29, ...), custom_call_target="tpu_custom_call" | custom-call | flops 671088640 | bytes 1048576 | tf_op jit(solution)/shard_map/rollout/pallas_call | solution.py:227
  52.0 1.0 %finish.1 = (f32[1,1024]{1,0:T(1,128)}, f32[128,1024]{1,0:T(8,128)}) custom-call(f32[136,256]{1,0:T(8,128)S(1)} %combine.7.mine_ref, f32[136,256]{1,0:T(8,128)S(1)} %collective-permute-done.8.got_ref, f32[128,256]{1,0:T(8,128)S(1)} %slice_add_fusion.2.refs_0_, f32[128,256]{1,0:T(8,128)S(1)} %collective-permute-done.10.refs_1_, ...), custom_call_target="tpu_custom_call" | custom-call | tf_op jit(solution)/shard_map/finish/pallas_call | solution.py:264
  (28 shorter events, 0.4 us)
Async XLA Ops:
  2.7 2.3 %collective-permute-start.3 = (f32[520,256]{1,0:T(8,128)S(1)}, f32[520,256]{1,0:T(8,128)S(1)}, u32[]{:S(2)}, u32[]{:S(2)}) collective-permute-start(f32[520,256]{1,0:T(8,128)S(1)} %get-tuple-element.40.refs_2_), channel_id=1, source_target_pairs={{0,1},{1,0},{2,3},{3,2},{4,5},{5,4},{6,7},{7,6},{8,9},{9,8},{10,11... | collective-permute-start | bytes 1597448 | tf_op jit(solution)/shard_map/ppermute | solution.py:281
  4.0 6.2 %collective-permute-start = (f32[1024,256]{1,0:T(8,128)S(1)}, f32[1024,256]{1,0:T(8,128)S(1)}, u32[]{:S(2)}, u32[]{:S(2)}) collective-permute-start(f32[1024,256]{1,0:T(8,128)S(1)} %get-tuple-element.35), channel_id=1, source_target_pairs={{0,1},{1,0},{2,3},{3,2},{4,5},{5,4},{6,7},{7,6},{8,9},{9,8},{10,11... | collective-permute-start | bytes 3145736 | tf_op jit(solution)/shard_map/ppermute | solution.py:281
  4.1 3.7 %collective-permute-start.1 = (f32[512,256]{1,0:T(8,128)S(1)}, f32[512,256]{1,0:T(8,128)S(1)}, u32[]{:S(2)}, u32[]{:S(2)}) collective-permute-start(f32[512,256]{1,0:T(8,128)S(1)} %get-tuple-element.37), channel_id=1, source_target_pairs={{0,1},{1,0},{2,3},{3,2},{4,5},{5,4},{6,7},{7,6},{8,9},{9,8},{10,11... | collective-permute-start | bytes 1572872 | tf_op jit(solution)/shard_map/ppermute | solution.py:281
  5.1 9.9 %collective-permute-start.4 = (f32[520,256]{1,0:T(8,128)S(1)}, f32[520,256]{1,0:T(8,128)S(1)}, u32[]{:S(2)}, u32[]{:S(2)}) collective-permute-start(f32[520,256]{1,0:T(8,128)S(1)} %combine.4.refs_3_), channel_id=1, source_target_pairs={{0,4},{1,3},{2,6},{3,1},{4,0},{5,7},{6,2},{7,5},{8,12},{9,11},{10,... | collective-permute-start | bytes 1597448 | tf_op jit(solution)/shard_map/ppermute | solution.py:281
  7.8 15.9 %collective-permute-start.2 = (f32[512,256]{1,0:T(8,128)S(1)}, f32[512,256]{1,0:T(8,128)S(1)}, u32[]{:S(2)}, u32[]{:S(2)}) collective-permute-start(f32[512,256]{1,0:T(8,128)S(1)} %add.41), channel_id=1, source_target_pairs={{0,4},{1,3},{2,6},{3,1},{4,0},{5,7},{6,2},{7,5},{8,12},{9,11},{10,... | collective-permute-start | bytes 1572872 | tf_op jit(solution)/shard_map/ppermute | solution.py:281
  15.1 8.7 %collective-permute-start.6 = (f32[264,256]{1,0:T(8,128)S(1)}, f32[264,256]{1,0:T(8,128)S(1)}, u32[]{:S(2)}, u32[]{:S(2)}) collective-permute-start(f32[264,256]{1,0:T(8,128)S(1)} %combine.5.refs_4_), channel_id=1, source_target_pairs={{0,2},{1,5},{2,0},{3,7},{4,6},{5,1},{6,4},{7,3},{8,10},{9,13},{10,... | collective-permute-start | bytes 811016 | tf_op jit(solution)/shard_map/ppermute | solution.py:281
  17.2 0.7 %copy-start.5 = (bf16[32,256]{1,0:T(8,128)(2,1)S(1)}, bf16[32,256]{1,0:T(8,128)(2,1)}, u32[]{:S(2)}) copy-start(bf16[32,256]{1,0:T(8,128)(2,1)} %param.12) | copy-start | bytes 49156
  17.2 9.1 %collective-permute-start.5 = (f32[256,256]{1,0:T(8,128)S(1)}, f32[256,256]{1,0:T(8,128)S(1)}, u32[]{:S(2)}, u32[]{:S(2)}) collective-permute-start(f32[256,256]{1,0:T(8,128)S(1)} %slice_add_fusion), channel_id=1, source_target_pairs={{0,2},{1,5},{2,0},{3,7},{4,6},{5,1},{6,4},{7,3},{8,10},{9,13},{10,... | collective-permute-start | bytes 786440 | tf_op jit(solution)/shard_map/ppermute | solution.py:281
  23.7 6.5 %collective-permute-start.7 = (f32[136,256]{1,0:T(8,128)S(1)}, f32[136,256]{1,0:T(8,128)S(1)}, u32[]{:S(2)}, u32[]{:S(2)}) collective-permute-start(f32[136,256]{1,0:T(8,128)S(1)} %combine.6.refs_5_), channel_id=1, source_target_pairs={{0,8},{1,17},{2,10},{3,19},{4,12},{5,21},{6,14},{7,23},{8,0},{9,25... | collective-permute-start | bytes 417800 | tf_op jit(solution)/shard_map/ppermute | solution.py:281
  26.3 11.7 %collective-permute-start.9 = (f32[128,256]{1,0:T(8,128)S(1)}, f32[128,256]{1,0:T(8,128)S(1)}, u32[]{:S(2)}, u32[]{:S(2)}) collective-permute-start(f32[128,256]{1,0:T(8,128)S(1)} %slice_add_fusion.3), channel_id=1, source_target_pairs={{0,8},{1,17},{2,10},{3,19},{4,12},{5,21},{6,14},{7,23},{8,0},{9,25... | collective-permute-start | bytes 393224 | tf_op jit(solution)/shard_map/ppermute | solution.py:281
  30.3 7.6 %collective-permute-start.8 = (f32[136,256]{1,0:T(8,128)S(1)}, f32[136,256]{1,0:T(8,128)S(1)}, u32[]{:S(2)}, u32[]{:S(2)}) collective-permute-start(f32[136,256]{1,0:T(8,128)S(1)} %combine.7.mine_ref), channel_id=1, source_target_pairs={{0,16},{1,9},{2,18},{3,11},{4,20},{5,13},{6,22},{7,15},{8,24},{9,1... | collective-permute-start | bytes 417800 | tf_op jit(solution)/shard_map/ppermute | solution.py:281
  33.4 0.9 %copy-start = (bf16[256,256]{1,0:T(8,128)(2,1)S(1)}, bf16[256,256]{1,0:T(8,128)(2,1)}, u32[]{:S(2)}) copy-start(bf16[256,256]{1,0:T(8,128)(2,1)} %ws_ref.15) | copy-start | bytes 393220
  33.4 1.0 %copy-start.1 = (bf16[256,256]{1,0:T(8,128)(2,1)S(1)}, bf16[256,256]{1,0:T(8,128)(2,1)}, u32[]{:S(2)}) copy-start(bf16[256,256]{1,0:T(8,128)(2,1)} %wo_ref.15) | copy-start | bytes 393220
  33.4 1.0 %copy-start.3 = (f32[256]{0:T(256)S(1)}, f32[256]{0:T(256)}, u32[]{:S(2)}) copy-start(f32[256]{0:T(256)} %param.15) | copy-start | bytes 3076
  33.5 1.0 %copy-start.4 = (f32[256]{0:T(256)S(1)}, f32[256]{0:T(256)}, u32[]{:S(2)}) copy-start(f32[256]{0:T(256)} %param.10) | copy-start | bytes 3076
  33.5 0.9 %copy-start.2 = (f32[256]{0:T(256)S(1)}, f32[256]{0:T(256)}, u32[]{:S(2)}) copy-start(f32[256]{0:T(256)} %param.13) | copy-start | bytes 3076
  38.0 6.9 %collective-permute-start.10 = (f32[128,256]{1,0:T(8,128)S(1)}, f32[128,256]{1,0:T(8,128)S(1)}, u32[]{:S(2)}, u32[]{:S(2)}) collective-permute-start(f32[128,256]{1,0:T(8,128)S(1)} %slice_add_fusion.2.refs_0_), channel_id=1, source_target_pairs={{0,2},{1,3},{2,0},{3,1},{4,6},{5,7},{6,4},{7,5},{8,10},{9,11},{10,... | collective-permute-start | bytes 393224 | tf_op jit(solution)/shard_map/ppermute | solution.py:281
  44.9 7.1 %collective-permute-start.11 = (f32[128,256]{1,0:T(8,128)S(1)}, f32[128,256]{1,0:T(8,128)S(1)}, u32[]{:S(2)}, u32[]{:S(2)}) collective-permute-start(f32[128,256]{1,0:T(8,128)S(1)} %slice_add_fusion.2.refs_0_), channel_id=1, source_target_pairs={{0,1},{1,0},{2,3},{3,2},{4,5},{5,4},{6,7},{7,6},{8,9},{9,8},{10,11... | collective-permute-start | bytes 393224 | tf_op jit(solution)/shard_map/ppermute | solution.py:281
  45.0 7.0 %collective-permute-start.12 = (f32[128,256]{1,0:T(8,128)S(1)}, f32[128,256]{1,0:T(8,128)S(1)}, u32[]{:S(2)}, u32[]{:S(2)}) collective-permute-start(f32[128,256]{1,0:T(8,128)S(1)} %collective-permute-done.10.refs_1_), channel_id=1, source_target_pairs={{0,1},{1,0},{2,3},{3,2},{4,5},{5,4},{6,7},{7,6},{8,9},{9,8},{10,11... | collective-permute-start | bytes 393224 | tf_op jit(solution)/shard_map/ppermute | solution.py:281
